TPU v7x, 32 devices: a whole 2x2x4 slice. The times are simulated.
32 devices in a mesh: clip: 4 (over z), row: 4 (over y, x), col: 2 (over core).
Axes of the slice: x: 2, y: 2, z: 4, core: 2. Of those that a mesh axis runs over, the one named last changes fastest.
Arguments:
- current: bfloat16 [4, 64, 32, 256], P('clip', 'row', 'col'), may hold values from -6 to 6
- bank: bfloat16 [4, 8, 64, 32, 256], P('clip', None, 'row', 'col'), may hold values from -6 to 6
- request: int32 [4, 15], replicated, may hold values from 0 to 15, as said below
- frame_pick: int32 [4, 15], replicated, may hold values from 0 to 7
- shift_rows: int32 [4, 15], replicated, may hold values from -1 to 1
- shift_cols: int32 [4, 15], replicated, may hold values from -1 to 1
- hist_count: int32 [4], replicated, may hold values from 1 to 15
- join_weight: bfloat16 [4096, 256], replicated, may hold values from -0.09375 to 0.09375
- conv_one: bfloat16 [2304, 256], replicated, may hold values from -0.125 to 0.125
- conv_two: bfloat16 [2304, 256], replicated, may hold values from -0.125 to 0.125
- grad_out: bfloat16 [4, 64, 32, 256], P('clip', 'row', 'col'), may hold values from -6 to 6
Outputs:
- encoded: bfloat16 [4, 64, 32, 256], P('clip', 'row', 'col')
- weight_grads: float32 [8704, 256], P(('clip', 'row'), 'col')
Inputs may be any that keep to these rules, and one draw needn't show every extreme that they name: `request`: each row holds 15 different values; value v names source clip v // 4, so at most 4 slots of one clip come from one source clip.
All inputs are finite; a program needn't handle non-finite values.
Results may differ from a plain program's by a relative error of at most 0.012.
The roundings to bfloat16 on the way count: a program that leaves them out, or rounds other values in their place, can miss the bound.
Values may be sent and summed in bfloat16 or wider, within the bound.
A program may use at most 128 MiB of HBM per device.

v0:
```python
import jax
import jax.numpy as jnp
from jax import lax
from jax.sharding import PartitionSpec as P

HIST = 15
TS = 8


def extended(block, sides, width):
    for axis, dim in sides:
        count = lax.axis_size(axis)
        forward = [(i, i + 1) for i in range(count - 1)]
        backward = [(target, source) for source, target in forward]
        low = lax.ppermute(
            lax.slice_in_dim(block, block.shape[dim] - width, None, axis=dim), axis, forward
        )
        high = lax.ppermute(lax.slice_in_dim(block, 0, width, axis=dim), axis, backward)
        block = jnp.concatenate([low, block, high], axis=dim)
    return block


def tap_views(padded, height, width, mirror):
    views = []
    for row_tap in range(3):
        for col_tap in range(3):
            top = 2 - row_tap if mirror else row_tap
            left = 2 - col_tap if mirror else col_tap
            views.append(padded[top : top + height, left : left + width])
    return jnp.concatenate(views, axis=-1).reshape(height * width, -1)


def forward_patch(field):
    padded = extended(field, (("row", 0), ("col", 1)), 1)
    return tap_views(padded, field.shape[0], field.shape[1], False)


def backward_patch(field):
    padded = extended(field, (("row", 0), ("col", 1)), 1)
    return tap_views(padded, field.shape[0], field.shape[1], True)


def flipped(weight):
    channels = weight.shape[1]
    return weight.reshape(9, channels, channels).transpose(0, 2, 1).reshape(9 * channels, channels)


def window_cut(padded, step_rows, step_cols, height, width, tile):
    start_row = (1 - step_rows) * tile
    start_col = (1 - step_cols) * tile
    zero = jnp.int32(0)
    return lax.dynamic_slice(padded, (start_row, start_col, zero), (height, width, padded.shape[2]))


def local(
    current,
    bank,
    request,
    frame_pick,
    shift_rows,
    shift_cols,
    hist_count,
    join_weight,
    conv_one,
    conv_two,
    grad_out,
):
    height, width, channels = (current.shape[1], current.shape[2], current.shape[3])
    clip_count = lax.axis_size("clip")
    capacity = (HIST + clip_count - 1) // clip_count
    own_clip = lax.axis_index("clip")
    slot_ids = own_clip * capacity + jnp.arange(capacity, dtype=jnp.int32)
    matches = (request[:, None, :] == slot_ids[None, :, None]).astype(jnp.int32)
    chosen = jnp.sum(matches * frame_pick[:, None, :], axis=-1).reshape(-1)
    served = jnp.sum(matches, axis=-1).reshape(-1).astype(jnp.bfloat16)
    own_request = lax.dynamic_index_in_dim(request, own_clip, 0, False)
    own_rows = lax.dynamic_index_in_dim(shift_rows, own_clip, 0, False)
    own_cols = lax.dynamic_index_in_dim(shift_cols, own_clip, 0, False)
    own_count = lax.dynamic_index_in_dim(hist_count, own_clip, 0, False)
    frames = bank[0]
    outgoing = jnp.take(frames, chosen, axis=0) * served[:, None, None, None]
    outgoing = outgoing.reshape(clip_count, capacity, height, width, channels)
    received = lax.all_to_all(outgoing, "clip", split_axis=0, concat_axis=0, tiled=True)
    fetched = jnp.take(
        received.reshape(clip_count * capacity, height, width, channels), own_request, axis=0
    )
    padded_slots = extended(fetched, (("row", 1), ("col", 2)), TS)
    warped = jax.vmap(
        lambda slot, step_rows, step_cols: window_cut(slot, step_rows, step_cols, height, width, TS)
    )(padded_slots, own_rows, own_cols)
    valid = (jnp.arange(HIST) < own_count).astype(jnp.bfloat16)
    warped = warped * valid[:, None, None, None]
    cells = height * width
    stacked = jnp.concatenate([current[0][None], warped], axis=0).reshape(HIST + 1, cells, channels)
    join_blocks = join_weight.reshape(HIST + 1, channels, channels)
    joined = jnp.einsum(
        "kpc,kcd->pd", stacked, join_blocks, preferred_element_type=jnp.float32
    ).astype(jnp.bfloat16)
    act = jnp.maximum(joined, 0)
    act_patch = forward_patch(act.reshape(height, width, channels))
    conv1 = jnp.dot(act_patch, conv_one, preferred_element_type=jnp.float32)
    hidden = jnp.maximum(conv1, 0.0).astype(jnp.bfloat16)
    hidden_patch = forward_patch(hidden.reshape(height, width, channels))
    conv2 = jnp.dot(hidden_patch, conv_two, preferred_element_type=jnp.float32)
    encoded = (
        (joined.astype(jnp.float32) + conv2)
        .astype(jnp.bfloat16)
        .reshape(1, height, width, channels)
    )
    upstream = grad_out[0]
    flat_up = upstream.reshape(cells, channels)
    grad_two = jnp.dot(hidden_patch.T, flat_up, preferred_element_type=jnp.float32)
    d_hidden = jnp.dot(
        backward_patch(upstream), flipped(conv_two), preferred_element_type=jnp.float32
    )
    d_conv1 = jnp.where(conv1 > 0, d_hidden, 0.0).astype(jnp.bfloat16)
    grad_one = jnp.dot(act_patch.T, d_conv1, preferred_element_type=jnp.float32)
    d_act = jnp.dot(
        backward_patch(d_conv1.reshape(height, width, channels)),
        flipped(conv_one),
        preferred_element_type=jnp.float32,
    )
    d_joined = (flat_up.astype(jnp.float32) + jnp.where(joined > 0, d_act, 0.0)).astype(
        jnp.bfloat16
    )
    grad_join = jnp.einsum(
        "kpc,pd->kcd", stacked, d_joined, preferred_element_type=jnp.float32
    ).reshape((HIST + 1) * channels, channels)
    term = jnp.concatenate([grad_join, grad_one, grad_two], axis=0)
    shared = lax.psum_scatter(term, ("clip", "row"), scatter_dimension=0, tiled=True)
    weight_grads = lax.psum_scatter(
        shared.astype(jnp.bfloat16), "col", scatter_dimension=1, tiled=True
    ).astype(jnp.float32)
    return (encoded, weight_grads)


def solution(mesh):
    placed = (
        P("clip", "row", "col", None),
        P("clip", None, "row", "col", None),
        P(),
        P(),
        P(),
        P(),
        P(),
        P(),
        P(),
        P(),
        P("clip", "row", "col", None),
    )
    return jax.shard_map(
        local,
        mesh=mesh,
        in_specs=placed,
        out_specs=(P("clip", "row", "col", None), P(("clip", "row"), "col")),
        check_vma=False,
    )
```

profile of v0, /device:TPU:0, one launch (start us, length us, event | category | flops | bytes accessed | tf_op | source)
XLA Modules:
  0.0 458.0 jit_solution(6086454931011811057)
XLA Ops:
  7.2 1.1 fusion.11
  8.5 3.3 gather_fusion
  11.7 3.2 select_multiply_fusion
  14.9 6.5 %all-to-all-start = ((bf16[4,4,16,16,256]{4,3,2,1,0:T(8,128)(2,1)}), bf16[4,4,16,16,256]{4,3,2,1,0:T(8,128)(2,1)}, u32[]{:S(2)}, u32[]{:S(2)}) async-start(bf16[4,4,16,16,256]{4,3,2,1,0:T(8,128)(2,1)} %select_multiply_fusion), calls=%async_computation | async-start | bytes 4194304 | tf_op jit(solution)/shard_map/all_to_all | solution.py:83
  21.5 48.2 %all-to-all-done = bf16[4,4,16,16,256]{4,3,2,1,0:T(8,128)(2,1)} async-done(((bf16[4,4,16,16,256]{4,3,2,1,0:T(8,128)(2,1)}), bf16[4,4,16,16,256]{4,3,2,1,0:T(8,128)(2,1)}, u32[]{:S(2)}, u32[]{:S(2)}) %all-to-all-start) | async-done | bytes 2097184 | tf_op jit(solution)/shard_map/all_to_all | solution.py:83
  69.7 3.6 gather_fusion.1
  73.3 1.8 broadcast_select_fusion
  75.3 1.3 collective-permute-start.1
  76.6 4.6 %collective-permute-start = (bf16[15,8,16,256]{3,2,1,0:T(8,128)(2,1)S(1)}, bf16[15,8,16,256]{3,2,1,0:T(8,128)(2,1)S(1)}, u32[]{:S(2)}, u32[]{:S(2)}) collective-permute-start(bf16[15,8,16,256]{3,2,1,0:T(8,128)(2,1)S(1)} %get-tuple-element.6), channel_id=1, source_target_pairs={{0,2},{2,4},{4,6},{1,3},{3,5},{5,7},{8,10},{10,12},{12,14},{9,11},... | collective-permute-start | bytes 2949128 | tf_op jit(solution)/shard_map/ppermute | solution.py:15
  81.2 20.6 %collective-permute-done.1 = bf16[15,8,16,256]{3,2,1,0:T(8,128)(2,1)S(1)} collective-permute-done((bf16[15,8,16,256]{3,2,1,0:T(8,128)(2,1)S(1)}, bf16[15,8,16,256]{3,2,1,0:T(8,128)(2,1)S(1)}, u32[]{:S(2)}, u32[]{:S(2)}) %collective-permute-start.1) | collective-permute-done | bytes 983072 | tf_op jit(solution)/shard_map/ppermute | solution.py:18
  104.2 2.5 fusion.27
  106.7 1.3 collective-permute-start.3
  108.0 5.7 %collective-permute-start.2 = (bf16[15,32,8,256]{3,2,1,0:T(8,128)(2,1)}, bf16[15,32,8,256]{3,2,1,0:T(8,128)(2,1)}, u32[]{:S(2)}, u32[]{:S(2)}) collective-permute-start(bf16[15,32,8,256]{3,2,1,0:T(8,128)(2,1)} %get-tuple-element.4), channel_id=1, source_target_pairs={{0,1},{2,3},{4,5},{6,7},{8,9},{10,11},{12,13},{14,15},{16,17},{18,... | collective-permute-start | bytes 5898248 | tf_op jit(solution)/shard_map/ppermute | solution.py:15
  113.7 1.3 collective-permute-start.13
  115.0 20.3 %collective-permute-start.12 = (bf16[1,16,256]{2,1,0:T(8,128)(2,1)S(1)}, bf16[1,16,256]{2,1,0:T(8,128)(2,1)S(1)}, u32[]{:S(2)}, u32[]{:S(2)}) collective-permute-start(bf16[1,16,256]{2,1,0:T(8,128)(2,1)S(1)} %get-tuple-element.54), channel_id=1, source_target_pairs={{0,2},{2,4},{4,6},{1,3},{3,5},{5,7},{8,10},{10,12},{12,14},{9,11},... | collective-permute-start | bytes 24584 | tf_op jit(solution)/shard_map/ppermute | solution.py:15
  138.2 1.5 copy.35
  139.8 2.4 copy.36
  142.2 1.3 collective-permute-start.15
  143.5 1.3 collective-permute-start.14
  144.8 1.7 collective-permute-done.14
  149.1 6.9 %pad_maximum_fusion.1 = bf16[15,32,32,256]{3,2,1,0:T(8,128)(2,1)} fusion(bf16[15,32,8,256]{3,2,1,0:T(8,128)(2,1)} %collective-permute-done.3, bf16[15,8,16,256]{3,2,1,0:T(8,128)(2,1)S(1)} %copy-done.9, bf16[15,16,16,256]{3,2,1,0:T(8,128)(2,1)S(1)} %copy-done.2, bf16[15,8,16,256]{3,2,1,0:T(8,128)(2,1)S(1)} %copy-done.11, ...), kind=kLoop, calls=%fused_computation.4 | loop fusion | flops 39321600 | bytes 15728640 | tf_op jit(solution)/shard_map/concatenate | solution.py:19
  155.9 12.7 %copy.31 = bf16[15,32,32,256]{3,0,2,1:T(8,128)(2,1)} copy(bf16[15,32,32,256]{3,2,1,0:T(8,128)(2,1)} %pad_maximum_fusion.1) | data formatting | bytes 15728640 | tf_op jit(solution)/shard_map/concatenate | solution.py:19
  168.7 7.2 %gather_fusion.2 = bf16[15,16,16,256]{3,0,2,1:T(8,128)(2,1)} fusion(bf16[15,32,32,256]{3,0,2,1:T(8,128)(2,1)} %copy.31, s32[15]{0:T(128)S(1)} %fusion.24), kind=kCustom, calls=%fused_computation.2 | custom fusion | bytes 3932400 | tf_op jit(solution)/shard_map/vmap()/gather | solution.py:52
  175.9 1.8 broadcast_multiply_fusion
  180.1 1.4 broadcast_maximum_fusion
  182.1 1.3 collective-permute-start.5
  183.4 5.9 %collective-permute-start.4 = (bf16[1,16,256]{2,1,0:T(8,128)(2,1)}, bf16[1,16,256]{2,1,0:T(8,128)(2,1)S(1)}, u32[]{:S(2)}, u32[]{:S(2)}) collective-permute-start(bf16[1,16,256]{2,1,0:T(8,128)(2,1)} %get-tuple-element.62), channel_id=1, source_target_pairs={{0,2},{2,4},{4,6},{1,3},{3,5},{5,7},{8,10},{10,12},{12,14},{9,11},... | collective-permute-start | bytes 24584 | tf_op jit(solution)/shard_map/ppermute | solution.py:15
  189.3 4.3 copy.34
  193.7 1.3 collective-permute-start.7
  195.0 3.0 collective-permute-start.6
  200.8 1.3 collective-permute-start.9
  202.1 5.4 %collective-permute-start.8 = (bf16[1,16,256]{2,1,0:T(8,128)(2,1)S(1)}, bf16[1,16,256]{2,1,0:T(8,128)(2,1)S(1)}, u32[]{:S(2)}, u32[]{:S(2)}) collective-permute-start(bf16[1,16,256]{2,1,0:T(8,128)(2,1)S(1)} %get-tuple-element.58), channel_id=1, source_target_pairs={{0,2},{2,4},{4,6},{1,3},{3,5},{5,7},{8,10},{10,12},{12,14},{9,11},... | collective-permute-start | bytes 24584 | tf_op jit(solution)/shard_map/ppermute | solution.py:15
  208.1 1.9 fusion.37
  210.0 1.3 collective-permute-start.17
  211.3 5.4 %collective-permute-start.16 = (bf16[1,16,256]{2,1,0:T(8,128)(2,1)S(1)}, bf16[1,16,256]{2,1,0:T(8,128)(2,1)S(1)}, u32[]{:S(2)}, u32[]{:S(2)}) collective-permute-start(bf16[1,16,256]{2,1,0:T(8,128)(2,1)S(1)} %get-tuple-element.50), channel_id=1, source_target_pairs={{0,2},{2,4},{4,6},{1,3},{3,5},{5,7},{8,10},{10,12},{12,14},{9,11},... | collective-permute-start | bytes 24584 | tf_op jit(solution)/shard_map/ppermute | solution.py:15
  216.8 1.3 collective-permute-start.11
  218.1 3.0 collective-permute-start.10
  221.2 1.3 collective-permute-start.19
  222.5 1.3 collective-permute-start.18
  224.3 1.9 fusion.38
  232.5 6.1 %fusion.5 = f32[4096,256]{1,0:T(8,128)} fusion(bf16[4096,256]{1,0:T(8,128)(2,1)} %bitcast.112, bf16[256,2304]{1,0:T(8,128)(2,1)} %constant_dynamic-update-slice_fusion.27, bf16[2304,256]{1,0:T(8,128)(2,1)} %bitcast.123, bf16[256,256]{1,0:T(8,128)(2,1)S(1)} %bitcast.119, bf16[256,256]{1,0:T(8,128)(2,1)S(1)} %copy-done.12), kind=kOutput, calls=%fused_computation.18 | convolution fusion | flops 839188480 | bytes 8912896 | tf_op jit(solution)/shard_map/kpc,pd->kcd/dot_general | solution.py:126
  238.6 8.2 %pad_maximum_fusion = f32[8704,256]{1,0:T(8,128)} fusion(f32[2304,256]{1,0:T(8,128)} %fusion.38, f32[2304,256]{1,0:T(8,128)} %fusion.37, f32[4096,256]{1,0:T(8,128)} %fusion.5), kind=kLoop, calls=%fused_computation.3 | loop fusion | flops 4456448 | bytes 17825792 | tf_op jit(solution)/shard_map/concatenate | solution.py:129
  246.9 188.3 %reduce-scatter.5.cloned.1.call-done = f32[544,256]{1,0:T(8,128)} async-done(((f32[8704,256]{1,0:T(8,128)}), f32[544,256]{1,0:T(8,128)}) %reduce-scatter.5.cloned.1.call-update) | async-done | bytes 557072 | tf_op jit(solution)/shard_map/reduce_scatter | solution.py:130
  435.2 1.8 convert_element_type.54
  437.0 1.9 copy.38
  438.9 2.4 fusion.1
  441.3 8.1 %reduce-scatter.7.cloned.1.call-done = bf16[128,544]{1,0:T(8,128)(2,1)} async-done(((bf16[256,544]{1,0:T(8,128)(2,1)}), bf16[128,544]{1,0:T(8,128)(2,1)}) %reduce-scatter.7.cloned.1.call-update) | async-done | bytes 139280
  449.4 1.0 copy.39
  (136 shorter events, 21.8 us)
Async XLA Ops:
  7.2 173.0 %copy-start = (bf16[4096,256]{1,0:T(8,128)(2,1)S(1)}, bf16[4096,256]{1,0:T(8,128)(2,1)}, u32[]{:S(2)}) copy-start(bf16[4096,256]{1,0:T(8,128)(2,1)} %param.18) | copy-start | bytes 6291460
  14.9 6.5 %copy-start.16 = (s32[4,15]{1,0:T(4,128)S(1)}, s32[4,15]{1,0:T(4,128)}, u32[]{:S(2)}) copy-start(s32[4,15]{1,0:T(4,128)} %param.13) | copy-start | bytes 724
  14.9 54.8 %all-to-all-start = ((bf16[4,4,16,16,256]{4,3,2,1,0:T(8,128)(2,1)}), bf16[4,4,16,16,256]{4,3,2,1,0:T(8,128)(2,1)}, u32[]{:S(2)}, u32[]{:S(2)}) async-start(bf16[4,4,16,16,256]{4,3,2,1,0:T(8,128)(2,1)} %select_multiply_fusion), calls=%async_computation | async-start | bytes 4194304 | tf_op jit(solution)/shard_map/all_to_all | solution.py:83
  21.4 413.8 %reduce-scatter.5.cloned.1.call-start = ((), (), s32[]{:S(2)}) async-start(), calls=%async_computation.3 | async-start | bytes 9469952 | tf_op jit(solution)/shard_map/reduce_scatter | solution.py:130
  75.1 26.7 %copy-start.1 = (bf16[15,16,16,256]{3,2,1,0:T(8,128)(2,1)}, bf16[15,16,16,256]{3,2,1,0:T(8,128)(2,1)S(1)}, u32[]{:S(2)}) copy-start(bf16[15,16,16,256]{3,2,1,0:T(8,128)(2,1)S(1)} %broadcast_select_fusion) | copy-start | bytes 5898244
  75.3 26.5 %collective-permute-start.1 = (bf16[15,8,16,256]{3,2,1,0:T(8,128)(2,1)S(1)}, bf16[15,8,16,256]{3,2,1,0:T(8,128)(2,1)S(1)}, u32[]{:S(2)}, u32[]{:S(2)}) collective-permute-start(bf16[15,8,16,256]{3,2,1,0:T(8,128)(2,1)S(1)} %get-tuple-element.7), channel_id=1, source_target_pairs={{2,0},{4,2},{6,4},{3,1},{5,3},{7,5},{10,8},{12,10},{14,12},{11,9},... | collective-permute-start | bytes 2949128 | tf_op jit(solution)/shard_map/ppermute | solution.py:18
  76.6 25.2 %collective-permute-start = (bf16[15,8,16,256]{3,2,1,0:T(8,128)(2,1)S(1)}, bf16[15,8,16,256]{3,2,1,0:T(8,128)(2,1)S(1)}, u32[]{:S(2)}, u32[]{:S(2)}) collective-permute-start(bf16[15,8,16,256]{3,2,1,0:T(8,128)(2,1)S(1)} %get-tuple-element.6), channel_id=1, source_target_pairs={{0,2},{2,4},{4,6},{1,3},{3,5},{5,7},{8,10},{10,12},{12,14},{9,11},... | collective-permute-start | bytes 2949128 | tf_op jit(solution)/shard_map/ppermute | solution.py:15
  101.8 1.0 copy-start.8
  102.7 1.0 copy-start.10
  104.2 9.5 %copy-start.4 = (bf16[1,16,16,256]{3,2,1,0:T(8,128)(2,1)S(1)}, bf16[1,16,16,256]{3,2,1,0:T(8,128)(2,1)}, u32[]{:S(2)}) copy-start(bf16[1,16,16,256]{3,2,1,0:T(8,128)(2,1)} %param.21) | copy-start | bytes 393220
  104.2 31.1 %copy-start.17 = (s32[4]{0:T(128)S(1)}, s32[4]{0:T(128)}, u32[]{:S(2)}) copy-start(s32[4]{0:T(128)} %param.17) | copy-start | bytes 52
  104.2 33.1 %copy-start.15 = (bf16[1,16,16,256]{3,2,1,0:T(8,128)(2,1)S(1)}, bf16[1,16,16,256]{3,2,1,0:T(8,128)(2,1)}, u32[]{:S(2)}) copy-start(bf16[1,16,16,256]{3,2,1,0:T(8,128)(2,1)} %param.11) | copy-start | bytes 393220
  104.2 34.0 %copy-start.5 = (bf16[2304,256]{1,0:T(8,128)(2,1)S(1)}, bf16[2304,256]{1,0:T(8,128)(2,1)}, u32[]{:S(2)}) copy-start(bf16[2304,256]{1,0:T(8,128)(2,1)} %param.20) | copy-start | bytes 3538948
  106.7 40.8 %collective-permute-start.3 = (bf16[15,32,8,256]{3,2,1,0:T(8,128)(2,1)}, bf16[15,32,8,256]{3,2,1,0:T(8,128)(2,1)}, u32[]{:S(2)}, u32[]{:S(2)}) collective-permute-start(bf16[15,32,8,256]{3,2,1,0:T(8,128)(2,1)} %get-tuple-element.5), channel_id=1, source_target_pairs={{1,0},{3,2},{5,4},{7,6},{9,8},{11,10},{13,12},{15,14},{17,16},{19,... | collective-permute-start | bytes 5898248 | tf_op jit(solution)/shard_map/ppermute | solution.py:18
  108.0 39.5 %collective-permute-start.2 = (bf16[15,32,8,256]{3,2,1,0:T(8,128)(2,1)}, bf16[15,32,8,256]{3,2,1,0:T(8,128)(2,1)}, u32[]{:S(2)}, u32[]{:S(2)}) collective-permute-start(bf16[15,32,8,256]{3,2,1,0:T(8,128)(2,1)} %get-tuple-element.4), channel_id=1, source_target_pairs={{0,1},{2,3},{4,5},{6,7},{8,9},{10,11},{12,13},{14,15},{16,17},{18,... | collective-permute-start | bytes 5898248 | tf_op jit(solution)/shard_map/ppermute | solution.py:15
  113.7 28.5 %collective-permute-start.13 = (bf16[1,16,256]{2,1,0:T(8,128)(2,1)S(1)}, bf16[1,16,256]{2,1,0:T(8,128)(2,1)S(1)}, u32[]{:S(2)}, u32[]{:S(2)}) collective-permute-start(bf16[1,16,256]{2,1,0:T(8,128)(2,1)S(1)} %get-tuple-element.55), channel_id=1, source_target_pairs={{2,0},{4,2},{6,4},{3,1},{5,3},{7,5},{10,8},{12,10},{14,12},{11,9},... | collective-permute-start | bytes 24584 | tf_op jit(solution)/shard_map/ppermute | solution.py:18
  115.0 27.2 %collective-permute-start.12 = (bf16[1,16,256]{2,1,0:T(8,128)(2,1)S(1)}, bf16[1,16,256]{2,1,0:T(8,128)(2,1)S(1)}, u32[]{:S(2)}, u32[]{:S(2)}) collective-permute-start(bf16[1,16,256]{2,1,0:T(8,128)(2,1)S(1)} %get-tuple-element.54), channel_id=1, source_target_pairs={{0,2},{2,4},{4,6},{1,3},{3,5},{5,7},{8,10},{10,12},{12,14},{9,11},... | collective-permute-start | bytes 24584 | tf_op jit(solution)/shard_map/ppermute | solution.py:15
  142.2 2.6 collective-permute-start.15
  143.5 3.1 collective-permute-start.14
  146.5 1.2 copy-start.11
  146.7 1.5 copy-start.9
  147.4 1.7 copy-start.2
  175.9 1.8 copy-start.13
  178.8 1.4 copy-start.3
  180.1 9.2 %copy-start.14 = (bf16[16,16,256]{2,1,0:T(8,128)(2,1)S(1)}, bf16[16,16,256]{2,1,0:T(8,128)(2,1)}, u32[]{:S(2)}) copy-start(bf16[16,16,256]{2,1,0:T(8,128)(2,1)} %get-tuple-element.14) | copy-start | bytes 393220
  182.1 11.5 %collective-permute-start.5 = (bf16[1,16,256]{2,1,0:T(8,128)(2,1)}, bf16[1,16,256]{2,1,0:T(8,128)(2,1)S(1)}, u32[]{:S(2)}, u32[]{:S(2)}) collective-permute-start(bf16[1,16,256]{2,1,0:T(8,128)(2,1)} %get-tuple-element.63), channel_id=1, source_target_pairs={{2,0},{4,2},{6,4},{3,1},{5,3},{7,5},{10,8},{12,10},{14,12},{11,9},... | collective-permute-start | bytes 24584 | tf_op jit(solution)/shard_map/ppermute | solution.py:18
  183.4 10.2 %collective-permute-start.4 = (bf16[1,16,256]{2,1,0:T(8,128)(2,1)}, bf16[1,16,256]{2,1,0:T(8,128)(2,1)S(1)}, u32[]{:S(2)}, u32[]{:S(2)}) collective-permute-start(bf16[1,16,256]{2,1,0:T(8,128)(2,1)} %get-tuple-element.62), channel_id=1, source_target_pairs={{0,2},{2,4},{4,6},{1,3},{3,5},{5,7},{8,10},{10,12},{12,14},{9,11},... | collective-permute-start | bytes 24584 | tf_op jit(solution)/shard_map/ppermute | solution.py:15
  193.7 4.4 collective-permute-start.7
  195.0 3.9 collective-permute-start.6
  198.9 0.9 copy-start.12
  199.0 1.3 copy-start.6
  200.3 7.3 %copy-start.7 = (bf16[9,256,256]{2,1,0:T(8,128)(2,1)S(1)}, bf16[9,256,256]{2,1,0:T(8,128)(2,1)}, u32[]{:S(2)}) copy-start(bf16[9,256,256]{2,1,0:T(8,128)(2,1)} %copy.35) | copy-start | bytes 3538948
  200.8 15.9 %collective-permute-start.9 = (bf16[1,16,256]{2,1,0:T(8,128)(2,1)S(1)}, bf16[1,16,256]{2,1,0:T(8,128)(2,1)S(1)}, u32[]{:S(2)}, u32[]{:S(2)}) collective-permute-start(bf16[1,16,256]{2,1,0:T(8,128)(2,1)S(1)} %get-tuple-element.59), channel_id=1, source_target_pairs={{2,0},{4,2},{6,4},{3,1},{5,3},{7,5},{10,8},{12,10},{14,12},{11,9},... | collective-permute-start | bytes 24584 | tf_op jit(solution)/shard_map/ppermute | solution.py:18
  202.1 14.7 %collective-permute-start.8 = (bf16[1,16,256]{2,1,0:T(8,128)(2,1)S(1)}, bf16[1,16,256]{2,1,0:T(8,128)(2,1)S(1)}, u32[]{:S(2)}, u32[]{:S(2)}) collective-permute-start(bf16[1,16,256]{2,1,0:T(8,128)(2,1)S(1)} %get-tuple-element.58), channel_id=1, source_target_pairs={{0,2},{2,4},{4,6},{1,3},{3,5},{5,7},{8,10},{10,12},{12,14},{9,11},... | collective-permute-start | bytes 24584 | tf_op jit(solution)/shard_map/ppermute | solution.py:15
  210.0 11.1 %collective-permute-start.17 = (bf16[1,16,256]{2,1,0:T(8,128)(2,1)S(1)}, bf16[1,16,256]{2,1,0:T(8,128)(2,1)S(1)}, u32[]{:S(2)}, u32[]{:S(2)}) collective-permute-start(bf16[1,16,256]{2,1,0:T(8,128)(2,1)S(1)} %get-tuple-element.51), channel_id=1, source_target_pairs={{2,0},{4,2},{6,4},{3,1},{5,3},{7,5},{10,8},{12,10},{14,12},{11,9},... | collective-permute-start | bytes 24584 | tf_op jit(solution)/shard_map/ppermute | solution.py:18
  211.3 9.9 %collective-permute-start.16 = (bf16[1,16,256]{2,1,0:T(8,128)(2,1)S(1)}, bf16[1,16,256]{2,1,0:T(8,128)(2,1)S(1)}, u32[]{:S(2)}, u32[]{:S(2)}) collective-permute-start(bf16[1,16,256]{2,1,0:T(8,128)(2,1)S(1)} %get-tuple-element.50), channel_id=1, source_target_pairs={{0,2},{2,4},{4,6},{1,3},{3,5},{5,7},{8,10},{10,12},{12,14},{9,11},... | collective-permute-start | bytes 24584 | tf_op jit(solution)/shard_map/ppermute | solution.py:15
  216.8 7.1 %collective-permute-start.11 = (bf16[18,1,256]{2,1,0:T(2,128)(2,1)S(1)}, bf16[18,1,256]{2,1,0:T(2,128)(2,1)S(1)}, u32[]{:S(2)}, u32[]{:S(2)}) collective-permute-start(bf16[18,1,256]{2,1,0:T(2,128)(2,1)S(1)} %get-tuple-element.42), channel_id=1, source_target_pairs={{1,0},{3,2},{5,4},{7,6},{9,8},{11,10},{13,12},{15,14},{17,16},{19,... | collective-permute-start | bytes 27656 | tf_op jit(solution)/shard_map/ppermute | solution.py:18
  218.1 5.8 %collective-permute-start.10 = (bf16[18,1,256]{2,1,0:T(2,128)(2,1)S(1)}, bf16[18,1,256]{2,1,0:T(2,128)(2,1)S(1)}, u32[]{:S(2)}, u32[]{:S(2)}) collective-permute-start(bf16[18,1,256]{2,1,0:T(2,128)(2,1)S(1)} %get-tuple-element.43), channel_id=1, source_target_pairs={{0,1},{2,3},{4,5},{6,7},{8,9},{10,11},{12,13},{14,15},{16,17},{18,... | collective-permute-start | bytes 27656 | tf_op jit(solution)/shard_map/ppermute | solution.py:15
  221.2 5.0 %collective-permute-start.19 = (bf16[18,1,256]{2,1,0:T(2,128)(2,1)S(1)}, bf16[18,1,256]{2,1,0:T(2,128)(2,1)S(1)}, u32[]{:S(2)}, u32[]{:S(2)}) collective-permute-start(bf16[18,1,256]{2,1,0:T(2,128)(2,1)S(1)} %get-tuple-element.34), channel_id=1, source_target_pairs={{0,1},{2,3},{4,5},{6,7},{8,9},{10,11},{12,13},{14,15},{16,17},{18,... | collective-permute-start | bytes 27656 | tf_op jit(solution)/shard_map/ppermute | solution.py:15
  222.5 3.7 collective-permute-start.18
  246.8 202.5 %reduce-scatter.7.cloned.1.call-start = ((), (), s32[]{:S(2)}) async-start(), calls=%async_computation.4 | async-start | bytes 491520
Sparse Core Ops, SparseCore 0:
  247.0 188.1 reduce-scatter.4
  439.0 10.3 reduce-scatter.6
where the time goes:
time: 459 us; the launch traced here: 458 us
  waiting for transfers between devices  268 us (58%)
  starting transfers between devices  75.5 us (16%)
  local copies, waits for them, and re-layouts  56 us (12%)
  other arithmetic  29.2 us (6%)
  between operations  14.9 us (3%)
  matrix products  14.7 us (3%)
    reduce_scatter x1, waiting for transfers between devices, local(): lax.psum_scatter(term, ('clip', 'row'), scatter_dimension=0, tiled=True)  188 us
    ppermute x10, starting transfers between devices, extended(): lax.ppermute(lax.slice_in_dim(block, block.shape[dim] - width, None, axis...  56.1 us
    all_to_all x1, waiting for transfers between devices, local(): lax.all_to_all(outgoing, 'clip', split_axis=0, concat_axis=0, tiled=True)  48.2 us
    ppermute x10, waiting for transfers between devices, extended(): lax.ppermute(lax.slice_in_dim(block, 0, width, axis=dim), axis, backward)  22.4 us
    unnamed x70, local copies, waits for them, and re-layouts  14.5 us
    ppermute x10, starting transfers between devices, extended(): lax.ppermute(lax.slice_in_dim(block, 0, width, axis=dim), axis, backward)  12.9 us
    concatenate x1, local copies, waits for them, and re-layouts, extended(): block = jnp.concatenate([low, block, high], axis=dim)  12.7 us
  transfers between devices with their start and end apart: 23, of which 6 were waited for; matrix products, arithmetic and copies ran while one was open for 4% of the time, Pallas kernels for 0%

commit v1 on v0

--- a/solution.py
+++ b/solution.py
@@ -127,9 +127,11 @@
         "kpc,pd->kcd", stacked, d_joined, preferred_element_type=jnp.float32
     ).reshape((HIST + 1) * channels, channels)
     term = jnp.concatenate([grad_join, grad_one, grad_two], axis=0)
-    shared = lax.psum_scatter(term, ("clip", "row"), scatter_dimension=0, tiled=True)
+    shared = lax.psum_scatter(
+        term.astype(jnp.bfloat16), "col", scatter_dimension=1, tiled=True
+    )
     weight_grads = lax.psum_scatter(
-        shared.astype(jnp.bfloat16), "col", scatter_dimension=1, tiled=True
+        shared, ("clip", "row"), scatter_dimension=0, tiled=True
     ).astype(jnp.float32)
     return (encoded, weight_grads)
 

time: 459 us -> 361 us (0.79)
  waiting for transfers between devices: 268 us -> 188 us
  starting transfers between devices: 75.5 us -> 52.2 us
  local copies, waits for them, and re-layouts: 56 us -> 63.7 us
    reduce_scatter x1, waiting for transfers between devices: 188 us -> 80.7 us  [local(): lax.psum_scatter(shared, ('clip', 'row'), scatter_dimension=0, tiled=True)]
    ppermute x10, starting transfers between devices: 56.1 us -> 32.8 us  [extended(): lax.ppermute(lax.slice_in_dim(block, block.shape[dim] - width, None, axis...]
    ppermute x10, waiting for transfers between devices: 0.81 us -> 19.7 us  [extended(): lax.ppermute(lax.slice_in_dim(block, block.shape[dim] - width, None, axis...]
    unnamed x70, local copies, waits for them, and re-layouts: 14.5 us -> 22.3 us
    unnamed x3, waiting for transfers between devices: 8.13 us -> 13.7 us
  transfers between devices with their start and end apart: 23 -> 23, of which waited for: 6 -> 9; matrix products, arithmetic and copies ran while one was open for 4% -> 5% of each run, Pallas kernels for 0% -> 0%
where the time goes in v1:
time: 361 us; the launch traced here: 359 us
  waiting for transfers between devices  188 us (52%)
  local copies, waits for them, and re-layouts  63.7 us (18%)
  starting transfers between devices  52.2 us (14%)
  other arithmetic  27.1 us (8%)
  between operations  14.9 us (4%)
  matrix products  13.3 us (4%)
    reduce_scatter x1, waiting for transfers between devices, local(): lax.psum_scatter(shared, ('clip', 'row'), scatter_dimension=0, tiled=True)  80.7 us
    all_to_all x1, waiting for transfers between devices, local(): lax.all_to_all(outgoing, 'clip', split_axis=0, concat_axis=0, tiled=True)  48.2 us
    ppermute x10, starting transfers between devices, extended(): lax.ppermute(lax.slice_in_dim(block, block.shape[dim] - width, None, axis...  32.8 us
    ppermute x10, waiting for transfers between devices, extended(): lax.ppermute(lax.slice_in_dim(block, 0, width, axis=dim), axis, backward)  25.7 us
    unnamed x70, local copies, waits for them, and re-layouts  22.3 us
    ppermute x10, waiting for transfers between devices, extended(): lax.ppermute(lax.slice_in_dim(block, block.shape[dim] - width, None, axis...  19.7 us
    unnamed x3, waiting for transfers between devices  13.7 us
    ppermute x10, starting transfers between devices, extended(): lax.ppermute(lax.slice_in_dim(block, 0, width, axis=dim), axis, backward)  12.9 us
  transfers between devices with their start and end apart: 23, of which 9 were waited for; matrix products, arithmetic and copies ran while one was open for 5% of the time, Pallas kernels for 0%

profile of v1, /device:TPU:0, one launch (start us, length us, event | category | flops | bytes accessed | tf_op | source)
XLA Modules:
  0.0 359.1 jit_solution(7724970467328606138)
XLA Ops:
  8.5 3.3 gather_fusion
  11.7 3.2 select_multiply_fusion
  14.9 6.5 %all-to-all-start = ((bf16[4,4,16,16,256]{4,3,2,1,0:T(8,128)(2,1)}), bf16[4,4,16,16,256]{4,3,2,1,0:T(8,128)(2,1)}, u32[]{:S(2)}, u32[]{:S(2)}) async-start(bf16[4,4,16,16,256]{4,3,2,1,0:T(8,128)(2,1)} %select_multiply_fusion), calls=%async_computation | async-start | bytes 4194304 | tf_op jit(solution)/shard_map/all_to_all | solution.py:83
  21.5 48.2 %all-to-all-done = bf16[4,4,16,16,256]{4,3,2,1,0:T(8,128)(2,1)} async-done(((bf16[4,4,16,16,256]{4,3,2,1,0:T(8,128)(2,1)}), bf16[4,4,16,16,256]{4,3,2,1,0:T(8,128)(2,1)}, u32[]{:S(2)}, u32[]{:S(2)}) %all-to-all-start) | async-done | bytes 2097184 | tf_op jit(solution)/shard_map/all_to_all | solution.py:83
  69.7 3.6 gather_fusion.1
  73.3 1.8 broadcast_select_fusion
  75.3 3.5 collective-permute-start
  78.7 1.3 collective-permute-start.1
  80.0 18.9 %collective-permute-done = bf16[15,8,16,256]{3,2,1,0:T(8,128)(2,1)S(1)} collective-permute-done((bf16[15,8,16,256]{3,2,1,0:T(8,128)(2,1)S(1)}, bf16[15,8,16,256]{3,2,1,0:T(8,128)(2,1)S(1)}, u32[]{:S(2)}, u32[]{:S(2)}) %collective-permute-start) | collective-permute-done | bytes 983072 | tf_op jit(solution)/shard_map/ppermute | solution.py:15
  98.9 23.0 %collective-permute-done.1 = bf16[15,8,16,256]{3,2,1,0:T(8,128)(2,1)S(1)} collective-permute-done((bf16[15,8,16,256]{3,2,1,0:T(8,128)(2,1)S(1)}, bf16[15,8,16,256]{3,2,1,0:T(8,128)(2,1)S(1)}, u32[]{:S(2)}, u32[]{:S(2)}) %collective-permute-start.1) | collective-permute-done | bytes 983072 | tf_op jit(solution)/shard_map/ppermute | solution.py:18
  123.5 2.5 fusion.26
  125.9 2.6 collective-permute-start.2
  128.6 1.3 collective-permute-start.3
  129.9 3.4 collective-permute-start.12
  133.3 1.3 collective-permute-start.13
  137.5 1.5 copy.35
  139.0 2.4 copy.36
  141.4 1.3 collective-permute-start.14
  142.7 4.0 %collective-permute-start.15 = (bf16[18,1,256]{2,1,0:T(2,128)(2,1)S(1)}, bf16[18,1,256]{2,1,0:T(2,128)(2,1)S(1)}, u32[]{:S(2)}, u32[]{:S(2)}) collective-permute-start(bf16[18,1,256]{2,1,0:T(2,128)(2,1)S(1)} %get-tuple-element.38), channel_id=1, source_target_pairs={{0,1},{2,3},{4,5},{6,7},{8,9},{10,11},{12,13},{14,15},{16,17},{18,... | collective-permute-start | bytes 27656 | tf_op jit(solution)/shard_map/ppermute | solution.py:15
  150.1 6.9 %pad_maximum_fusion = bf16[15,32,32,256]{3,2,1,0:T(8,128)(2,1)} fusion(bf16[15,32,8,256]{3,2,1,0:T(8,128)(2,1)} %collective-permute-done.3, bf16[15,8,16,256]{3,2,1,0:T(8,128)(2,1)S(1)} %copy-done.11, bf16[15,16,16,256]{3,2,1,0:T(8,128)(2,1)S(1)} %copy-done.2, bf16[15,8,16,256]{3,2,1,0:T(8,128)(2,1)S(1)} %copy-done.9, ...), kind=kLoop, calls=%fused_computation.3 | loop fusion | flops 39321600 | bytes 15728640 | tf_op jit(solution)/shard_map/concatenate | solution.py:19
  157.0 12.7 %copy.31 = bf16[15,32,32,256]{3,0,2,1:T(8,128)(2,1)} copy(bf16[15,32,32,256]{3,2,1,0:T(8,128)(2,1)} %pad_maximum_fusion) | data formatting | bytes 15728640 | tf_op jit(solution)/shard_map/concatenate | solution.py:19
  169.7 7.1 %gather_fusion.2 = bf16[15,16,16,256]{3,0,2,1:T(8,128)(2,1)} fusion(bf16[15,32,32,256]{3,0,2,1:T(8,128)(2,1)} %copy.31, s32[15]{0:T(128)S(1)} %fusion.23), kind=kCustom, calls=%fused_computation.2 | custom fusion | bytes 3932400 | tf_op jit(solution)/shard_map/vmap()/gather | solution.py:52
  176.9 1.8 broadcast_multiply_fusion
  181.1 1.4 broadcast_maximum_fusion
  183.1 4.3 %collective-permute-start.4 = (bf16[1,16,256]{2,1,0:T(8,128)(2,1)}, bf16[1,16,256]{2,1,0:T(8,128)(2,1)S(1)}, u32[]{:S(2)}, u32[]{:S(2)}) collective-permute-start(bf16[1,16,256]{2,1,0:T(8,128)(2,1)} %get-tuple-element.62), channel_id=1, source_target_pairs={{0,2},{2,4},{4,6},{1,3},{3,5},{5,7},{8,10},{10,12},{12,14},{9,11},... | collective-permute-start | bytes 24584 | tf_op jit(solution)/shard_map/ppermute | solution.py:15
  187.4 1.3 collective-permute-start.5
  188.7 4.3 %copy.34 = bf16[16,256,256]{2,1,0:T(8,128)(2,1)} copy(bf16[16,256,256]{1,0,2:T(8,128)(2,1)} %bitcast.111) | data formatting | bytes 4194304 | tf_op jit(solution)/shard_map/kpc,pd->kcd/dot_general | solution.py:126
  193.2 1.8 collective-permute-start.6
  195.0 1.3 collective-permute-start.7
  196.3 1.7 collective-permute-done.7
  201.3 1.6 convolution_convert_fusion.2
  202.9 4.2 %collective-permute-start.16 = (bf16[1,16,256]{2,1,0:T(8,128)(2,1)S(1)}, bf16[1,16,256]{2,1,0:T(8,128)(2,1)S(1)}, u32[]{:S(2)}, u32[]{:S(2)}) collective-permute-start(bf16[1,16,256]{2,1,0:T(8,128)(2,1)S(1)} %get-tuple-element.50), channel_id=1, source_target_pairs={{0,2},{2,4},{4,6},{1,3},{3,5},{5,7},{8,10},{10,12},{12,14},{9,11},... | collective-permute-start | bytes 24584 | tf_op jit(solution)/shard_map/ppermute | solution.py:15
  207.2 1.3 collective-permute-start.17
  208.5 4.6 %collective-permute-start.8 = (bf16[1,16,256]{2,1,0:T(8,128)(2,1)S(1)}, bf16[1,16,256]{2,1,0:T(8,128)(2,1)S(1)}, u32[]{:S(2)}, u32[]{:S(2)}) collective-permute-start(bf16[1,16,256]{2,1,0:T(8,128)(2,1)S(1)} %get-tuple-element.58), channel_id=1, source_target_pairs={{0,2},{2,4},{4,6},{1,3},{3,5},{5,7},{8,10},{10,12},{12,14},{9,11},... | collective-permute-start | bytes 24584 | tf_op jit(solution)/shard_map/ppermute | solution.py:15
  213.2 1.3 collective-permute-start.9
  214.5 1.3 collective-permute-start.18
  215.8 3.0 collective-permute-start.19
  219.6 1.3 collective-permute-start.10
  220.9 1.3 collective-permute-start.11
  226.3 1.6 convolution_convert_fusion.1
  230.7 5.3 %convolution_convert_fusion = bf16[4096,256]{1,0:T(8,128)(2,1)} fusion(bf16[4096,256]{1,0:T(8,128)(2,1)} %bitcast.114, bf16[256,2304]{1,0:T(8,128)(2,1)} %constant_dynamic-update-slice_fusion.27, bf16[2304,256]{1,0:T(8,128)(2,1)} %bitcast.126, bf16[256,256]{1,0:T(8,128)(2,1)S(1)} %bitcast.123, bf16[256,256]{1,0:T(8,128)(2,1)S(1)} %copy-done.12), kind=kOutput, calls=%fused_computation.4 | convolution fusion | flops 840237056 | bytes 6815744 | tf_op jit(solution)/shard_map/kpc,pd->kcd/dot_general | solution.py:126
  236.0 7.0 %pad_maximum_fusion.1 = bf16[8704,256]{1,0:T(8,128)(2,1)} fusion(bf16[2304,256]{1,0:T(8,128)(2,1)} %convolution_convert_fusion.1, bf16[2304,256]{1,0:T(8,128)(2,1)} %convolution_convert_fusion.2, bf16[4096,256]{1,0:T(8,128)(2,1)} %convolution_convert_fusion), kind=kLoop, calls=%fused_computation.5 | loop fusion | flops 13369344 | bytes 8912896 | tf_op jit(solution)/shard_map/concatenate | solution.py:129
  243.0 6.6 %copy.38 = bf16[8704,256]{0,1:T(8,128)(2,1)} copy(bf16[8704,256]{1,0:T(8,128)(2,1)} %pad_maximum_fusion.1) | data formatting | bytes 8912896
  249.7 13.7 %reduce-scatter.7.cloned.1.call-done = bf16[128,8704]{1,0:T(8,128)(2,1)} async-done(((bf16[256,8704]{1,0:T(8,128)(2,1)}), bf16[128,8704]{1,0:T(8,128)(2,1)}) %reduce-scatter.7.cloned.1.call-update) | async-done | bytes 2228240
  263.4 4.2 %copy.39 = bf16[8704,128]{1,0:T(8,128)(2,1)} copy(bf16[8704,128]{0,1:T(8,128)(2,1)} %bitcast.132) | data formatting | bytes 4456448
  267.6 2.4 fusion.1
  270.0 80.7 %reduce-scatter.5.cloned.1.call-done = bf16[544,128]{1,0:T(8,128)(2,1)} async-done(((bf16[8704,128]{1,0:T(8,128)(2,1)}), bf16[544,128]{1,0:T(8,128)(2,1)}) %reduce-scatter.5.cloned.1.call-update) | async-done | bytes 139280 | tf_op jit(solution)/shard_map/reduce_scatter | solution.py:133
  350.6 1.6 convert_element_type.52
  (135 shorter events, 22.9 us)
Async XLA Ops:
  7.2 174.0 %copy-start = (bf16[4096,256]{1,0:T(8,128)(2,1)S(1)}, bf16[4096,256]{1,0:T(8,128)(2,1)}, u32[]{:S(2)}) copy-start(bf16[4096,256]{1,0:T(8,128)(2,1)} %param.18) | copy-start | bytes 6291460
  14.9 6.5 %copy-start.16 = (s32[4,15]{1,0:T(4,128)S(1)}, s32[4,15]{1,0:T(4,128)}, u32[]{:S(2)}) copy-start(s32[4,15]{1,0:T(4,128)} %param.13) | copy-start | bytes 724
  14.9 54.8 %all-to-all-start = ((bf16[4,4,16,16,256]{4,3,2,1,0:T(8,128)(2,1)}), bf16[4,4,16,16,256]{4,3,2,1,0:T(8,128)(2,1)}, u32[]{:S(2)}, u32[]{:S(2)}) async-start(bf16[4,4,16,16,256]{4,3,2,1,0:T(8,128)(2,1)} %select_multiply_fusion), calls=%async_computation | async-start | bytes 4194304 | tf_op jit(solution)/shard_map/all_to_all | solution.py:83
  21.4 241.9 %reduce-scatter.7.cloned.1.call-start = ((), (), s32[]{:S(2)}) async-start(), calls=%async_computation.4 | async-start | bytes 6684672
  75.1 46.8 %copy-start.1 = (bf16[15,16,16,256]{3,2,1,0:T(8,128)(2,1)}, bf16[15,16,16,256]{3,2,1,0:T(8,128)(2,1)S(1)}, u32[]{:S(2)}) copy-start(bf16[15,16,16,256]{3,2,1,0:T(8,128)(2,1)S(1)} %broadcast_select_fusion) | copy-start | bytes 5898244
  75.3 23.7 %collective-permute-start = (bf16[15,8,16,256]{3,2,1,0:T(8,128)(2,1)S(1)}, bf16[15,8,16,256]{3,2,1,0:T(8,128)(2,1)S(1)}, u32[]{:S(2)}, u32[]{:S(2)}) collective-permute-start(bf16[15,8,16,256]{3,2,1,0:T(8,128)(2,1)S(1)} %get-tuple-element.6), channel_id=1, source_target_pairs={{0,2},{2,4},{4,6},{1,3},{3,5},{5,7},{8,10},{10,12},{12,14},{9,11},... | collective-permute-start | bytes 2949128 | tf_op jit(solution)/shard_map/ppermute | solution.py:15
  78.7 43.2 %collective-permute-start.1 = (bf16[15,8,16,256]{3,2,1,0:T(8,128)(2,1)S(1)}, bf16[15,8,16,256]{3,2,1,0:T(8,128)(2,1)S(1)}, u32[]{:S(2)}, u32[]{:S(2)}) collective-permute-start(bf16[15,8,16,256]{3,2,1,0:T(8,128)(2,1)S(1)} %get-tuple-element.7), channel_id=1, source_target_pairs={{2,0},{4,2},{6,4},{3,1},{5,3},{7,5},{10,8},{12,10},{14,12},{11,9},... | collective-permute-start | bytes 2949128 | tf_op jit(solution)/shard_map/ppermute | solution.py:18
  98.9 23.0 %copy-start.8 = (bf16[15,8,16,256]{3,2,1,0:T(8,128)(2,1)}, bf16[15,8,16,256]{3,2,1,0:T(8,128)(2,1)S(1)}, u32[]{:S(2)}) copy-start(bf16[15,8,16,256]{3,2,1,0:T(8,128)(2,1)S(1)} %collective-permute-done) | copy-start | bytes 2949124
  122.0 1.0 copy-start.10
  123.4 6.4 %copy-start.4 = (bf16[1,16,16,256]{3,2,1,0:T(8,128)(2,1)S(1)}, bf16[1,16,16,256]{3,2,1,0:T(8,128)(2,1)}, u32[]{:S(2)}) copy-start(bf16[1,16,16,256]{3,2,1,0:T(8,128)(2,1)} %param.21) | copy-start | bytes 393220
  123.4 11.2 %copy-start.17 = (s32[4]{0:T(128)S(1)}, s32[4]{0:T(128)}, u32[]{:S(2)}) copy-start(s32[4]{0:T(128)} %param.17) | copy-start | bytes 52
  123.4 13.1 %copy-start.15 = (bf16[1,16,16,256]{3,2,1,0:T(8,128)(2,1)S(1)}, bf16[1,16,16,256]{3,2,1,0:T(8,128)(2,1)}, u32[]{:S(2)}) copy-start(bf16[1,16,16,256]{3,2,1,0:T(8,128)(2,1)} %param.11) | copy-start | bytes 393220
  123.4 14.1 %copy-start.5 = (bf16[2304,256]{1,0:T(8,128)(2,1)S(1)}, bf16[2304,256]{1,0:T(8,128)(2,1)}, u32[]{:S(2)}) copy-start(bf16[2304,256]{1,0:T(8,128)(2,1)} %param.20) | copy-start | bytes 3538948
  125.9 22.6 %collective-permute-start.2 = (bf16[15,32,8,256]{3,2,1,0:T(8,128)(2,1)}, bf16[15,32,8,256]{3,2,1,0:T(8,128)(2,1)}, u32[]{:S(2)}, u32[]{:S(2)}) collective-permute-start(bf16[15,32,8,256]{3,2,1,0:T(8,128)(2,1)} %get-tuple-element.4), channel_id=1, source_target_pairs={{0,1},{2,3},{4,5},{6,7},{8,9},{10,11},{12,13},{14,15},{16,17},{18,... | collective-permute-start | bytes 5898248 | tf_op jit(solution)/shard_map/ppermute | solution.py:15
  128.6 20.0 %collective-permute-start.3 = (bf16[15,32,8,256]{3,2,1,0:T(8,128)(2,1)}, bf16[15,32,8,256]{3,2,1,0:T(8,128)(2,1)}, u32[]{:S(2)}, u32[]{:S(2)}) collective-permute-start(bf16[15,32,8,256]{3,2,1,0:T(8,128)(2,1)} %get-tuple-element.5), channel_id=1, source_target_pairs={{1,0},{3,2},{5,4},{7,6},{9,8},{11,10},{13,12},{15,14},{17,16},{19,... | collective-permute-start | bytes 5898248 | tf_op jit(solution)/shard_map/ppermute | solution.py:18
  129.9 11.5 %collective-permute-start.12 = (bf16[1,16,256]{2,1,0:T(8,128)(2,1)S(1)}, bf16[1,16,256]{2,1,0:T(8,128)(2,1)S(1)}, u32[]{:S(2)}, u32[]{:S(2)}) collective-permute-start(bf16[1,16,256]{2,1,0:T(8,128)(2,1)S(1)} %get-tuple-element.54), channel_id=1, source_target_pairs={{0,2},{2,4},{4,6},{1,3},{3,5},{5,7},{8,10},{10,12},{12,14},{9,11},... | collective-permute-start | bytes 24584 | tf_op jit(solution)/shard_map/ppermute | solution.py:15
  133.3 8.1 %collective-permute-start.13 = (bf16[1,16,256]{2,1,0:T(8,128)(2,1)S(1)}, bf16[1,16,256]{2,1,0:T(8,128)(2,1)S(1)}, u32[]{:S(2)}, u32[]{:S(2)}) collective-permute-start(bf16[1,16,256]{2,1,0:T(8,128)(2,1)S(1)} %get-tuple-element.55), channel_id=1, source_target_pairs={{2,0},{4,2},{6,4},{3,1},{5,3},{7,5},{10,8},{12,10},{14,12},{11,9},... | collective-permute-start | bytes 24584 | tf_op jit(solution)/shard_map/ppermute | solution.py:18
  141.4 5.4 %collective-permute-start.14 = (bf16[18,1,256]{2,1,0:T(2,128)(2,1)S(1)}, bf16[18,1,256]{2,1,0:T(2,128)(2,1)S(1)}, u32[]{:S(2)}, u32[]{:S(2)}) collective-permute-start(bf16[18,1,256]{2,1,0:T(2,128)(2,1)S(1)} %get-tuple-element.39), channel_id=1, source_target_pairs={{1,0},{3,2},{5,4},{7,6},{9,8},{11,10},{13,12},{15,14},{17,16},{19,... | collective-permute-start | bytes 27656 | tf_op jit(solution)/shard_map/ppermute | solution.py:18
  142.7 4.8 %collective-permute-start.15 = (bf16[18,1,256]{2,1,0:T(2,128)(2,1)S(1)}, bf16[18,1,256]{2,1,0:T(2,128)(2,1)S(1)}, u32[]{:S(2)}, u32[]{:S(2)}) collective-permute-start(bf16[18,1,256]{2,1,0:T(2,128)(2,1)S(1)} %get-tuple-element.38), channel_id=1, source_target_pairs={{0,1},{2,3},{4,5},{6,7},{8,9},{10,11},{12,13},{14,15},{16,17},{18,... | collective-permute-start | bytes 27656 | tf_op jit(solution)/shard_map/ppermute | solution.py:15
  147.6 1.2 copy-start.11
  147.7 1.5 copy-start.9
  148.4 1.7 copy-start.2
  176.9 1.8 copy-start.13
  179.8 1.4 copy-start.3
  181.1 7.5 %copy-start.14 = (bf16[16,16,256]{2,1,0:T(8,128)(2,1)S(1)}, bf16[16,16,256]{2,1,0:T(8,128)(2,1)}, u32[]{:S(2)}) copy-start(bf16[16,16,256]{2,1,0:T(8,128)(2,1)} %get-tuple-element.14) | copy-start | bytes 393220
  183.1 9.9 %collective-permute-start.4 = (bf16[1,16,256]{2,1,0:T(8,128)(2,1)}, bf16[1,16,256]{2,1,0:T(8,128)(2,1)S(1)}, u32[]{:S(2)}, u32[]{:S(2)}) collective-permute-start(bf16[1,16,256]{2,1,0:T(8,128)(2,1)} %get-tuple-element.62), channel_id=1, source_target_pairs={{0,2},{2,4},{4,6},{1,3},{3,5},{5,7},{8,10},{10,12},{12,14},{9,11},... | collective-permute-start | bytes 24584 | tf_op jit(solution)/shard_map/ppermute | solution.py:15
  187.4 5.8 %collective-permute-start.5 = (bf16[1,16,256]{2,1,0:T(8,128)(2,1)}, bf16[1,16,256]{2,1,0:T(8,128)(2,1)S(1)}, u32[]{:S(2)}, u32[]{:S(2)}) collective-permute-start(bf16[1,16,256]{2,1,0:T(8,128)(2,1)} %get-tuple-element.63), channel_id=1, source_target_pairs={{2,0},{4,2},{6,4},{3,1},{5,3},{7,5},{10,8},{12,10},{14,12},{11,9},... | collective-permute-start | bytes 24584 | tf_op jit(solution)/shard_map/ppermute | solution.py:18
  193.2 3.2 collective-permute-start.6
  195.0 3.1 collective-permute-start.7
  198.2 0.9 copy-start.12
  198.3 1.3 copy-start.6
  199.6 1.3 copy-start.7
  202.9 11.5 %collective-permute-start.16 = (bf16[1,16,256]{2,1,0:T(8,128)(2,1)S(1)}, bf16[1,16,256]{2,1,0:T(8,128)(2,1)S(1)}, u32[]{:S(2)}, u32[]{:S(2)}) collective-permute-start(bf16[1,16,256]{2,1,0:T(8,128)(2,1)S(1)} %get-tuple-element.50), channel_id=1, source_target_pairs={{0,2},{2,4},{4,6},{1,3},{3,5},{5,7},{8,10},{10,12},{12,14},{9,11},... | collective-permute-start | bytes 24584 | tf_op jit(solution)/shard_map/ppermute | solution.py:15
  207.2 7.3 %collective-permute-start.17 = (bf16[1,16,256]{2,1,0:T(8,128)(2,1)S(1)}, bf16[1,16,256]{2,1,0:T(8,128)(2,1)S(1)}, u32[]{:S(2)}, u32[]{:S(2)}) collective-permute-start(bf16[1,16,256]{2,1,0:T(8,128)(2,1)S(1)} %get-tuple-element.51), channel_id=1, source_target_pairs={{2,0},{4,2},{6,4},{3,1},{5,3},{7,5},{10,8},{12,10},{14,12},{11,9},... | collective-permute-start | bytes 24584 | tf_op jit(solution)/shard_map/ppermute | solution.py:18
  208.5 10.3 %collective-permute-start.8 = (bf16[1,16,256]{2,1,0:T(8,128)(2,1)S(1)}, bf16[1,16,256]{2,1,0:T(8,128)(2,1)S(1)}, u32[]{:S(2)}, u32[]{:S(2)}) collective-permute-start(bf16[1,16,256]{2,1,0:T(8,128)(2,1)S(1)} %get-tuple-element.58), channel_id=1, source_target_pairs={{0,2},{2,4},{4,6},{1,3},{3,5},{5,7},{8,10},{10,12},{12,14},{9,11},... | collective-permute-start | bytes 24584 | tf_op jit(solution)/shard_map/ppermute | solution.py:15
  213.2 6.4 %collective-permute-start.9 = (bf16[1,16,256]{2,1,0:T(8,128)(2,1)S(1)}, bf16[1,16,256]{2,1,0:T(8,128)(2,1)S(1)}, u32[]{:S(2)}, u32[]{:S(2)}) collective-permute-start(bf16[1,16,256]{2,1,0:T(8,128)(2,1)S(1)} %get-tuple-element.59), channel_id=1, source_target_pairs={{2,0},{4,2},{6,4},{3,1},{5,3},{7,5},{10,8},{12,10},{14,12},{11,9},... | collective-permute-start | bytes 24584 | tf_op jit(solution)/shard_map/ppermute | solution.py:18
  214.5 7.8 %collective-permute-start.18 = (bf16[18,1,256]{2,1,0:T(2,128)(2,1)S(1)}, bf16[18,1,256]{2,1,0:T(2,128)(2,1)S(1)}, u32[]{:S(2)}, u32[]{:S(2)}) collective-permute-start(bf16[18,1,256]{2,1,0:T(2,128)(2,1)S(1)} %get-tuple-element.35), channel_id=1, source_target_pairs={{1,0},{3,2},{5,4},{7,6},{9,8},{11,10},{13,12},{15,14},{17,16},{19,... | collective-permute-start | bytes 27656 | tf_op jit(solution)/shard_map/ppermute | solution.py:18
  215.8 6.5 %collective-permute-start.19 = (bf16[18,1,256]{2,1,0:T(2,128)(2,1)S(1)}, bf16[18,1,256]{2,1,0:T(2,128)(2,1)S(1)}, u32[]{:S(2)}, u32[]{:S(2)}) collective-permute-start(bf16[18,1,256]{2,1,0:T(2,128)(2,1)S(1)} %get-tuple-element.34), channel_id=1, source_target_pairs={{0,1},{2,3},{4,5},{6,7},{8,9},{10,11},{12,13},{14,15},{16,17},{18,... | collective-permute-start | bytes 27656 | tf_op jit(solution)/shard_map/ppermute | solution.py:15
  219.6 6.3 %collective-permute-start.10 = (bf16[18,1,256]{2,1,0:T(2,128)(2,1)S(1)}, bf16[18,1,256]{2,1,0:T(2,128)(2,1)S(1)}, u32[]{:S(2)}, u32[]{:S(2)}) collective-permute-start(bf16[18,1,256]{2,1,0:T(2,128)(2,1)S(1)} %get-tuple-element.43), channel_id=1, source_target_pairs={{0,1},{2,3},{4,5},{6,7},{8,9},{10,11},{12,13},{14,15},{16,17},{18,... | collective-permute-start | bytes 27656 | tf_op jit(solution)/shard_map/ppermute | solution.py:15
  220.9 5.0 %collective-permute-start.11 = (bf16[18,1,256]{2,1,0:T(2,128)(2,1)S(1)}, bf16[18,1,256]{2,1,0:T(2,128)(2,1)S(1)}, u32[]{:S(2)}, u32[]{:S(2)}) collective-permute-start(bf16[18,1,256]{2,1,0:T(2,128)(2,1)S(1)} %get-tuple-element.42), channel_id=1, source_target_pairs={{1,0},{3,2},{5,4},{7,6},{9,8},{11,10},{13,12},{15,14},{17,16},{19,... | collective-permute-start | bytes 27656 | tf_op jit(solution)/shard_map/ppermute | solution.py:18
  249.7 101.0 %reduce-scatter.5.cloned.1.call-start = ((), (), s32[]{:S(2)}) async-start(), calls=%async_computation.3 | async-start | bytes 2367488 | tf_op jit(solution)/shard_map/reduce_scatter | solution.py:133
Sparse Core Ops, SparseCore 0:
  249.8 13.5 reduce-scatter.6
  267.7 82.9 reduce-scatter.4

commit v2 on v1

--- a/solution.py
+++ b/solution.py
@@ -1,10 +1,11 @@
 import jax
 import jax.numpy as jnp
 from jax import lax
+from jax.experimental import pallas as pl
+from jax.experimental.pallas import tpu as pltpu
 from jax.sharding import PartitionSpec as P
 
 HIST = 15
-TS = 8
 
 
 def extended(block, sides, width):
@@ -20,6 +21,201 @@
     return block
 
 
+def fetch_kernel(
+    served, wanted, bank, out, own, rim, chosen, got, near_sem, row_sem, col_sem, clip_sem, local_sem
+):
+    frames = bank.shape[0]
+    clips = lax.axis_size("clip")
+    rows = lax.axis_size("row")
+    cols = lax.axis_size("col")
+    capacity = got.shape[1] // clips
+    clip = lax.axis_index("clip")
+    row = lax.axis_index("row")
+    col = lax.axis_index("col")
+    up, down, left, right = row > 0, row < rows - 1, col > 0, col < cols - 1
+
+    def signal(**where):
+        pl.semaphore_signal(
+            pltpu.get_barrier_semaphore(), inc=1, device_id=where, device_id_type=pl.DeviceIdType.MESH
+        )
+
+    def remote(source, target, sems, where):
+        return pltpu.make_async_remote_copy(
+            src_ref=source,
+            dst_ref=target,
+            send_sem=sems.at[0],
+            recv_sem=sems.at[1],
+            device_id=where,
+            device_id_type=pl.DeviceIdType.MESH,
+        )
+
+    centre = pltpu.make_async_copy(bank, own.at[0:frames, :, :, 1:3], local_sem)
+    centre.start()
+    partners = [lax.rem(clip + step, clips) for step in range(1, clips)]
+    for partner in partners:
+        signal(clip=partner)
+    for there, axis, index in (
+        (up, "row", row - 1),
+        (down, "row", row + 1),
+        (left, "col", col - 1),
+        (right, "col", col + 1),
+    ):
+        pl.when(there)(lambda axis=axis, index=index: signal(**{axis: index}))
+    peers = clips - 1
+    for there in (up, down, left, right):
+        peers = peers + there.astype(jnp.int32)
+    pl.semaphore_wait(pltpu.get_barrier_semaphore(), peers)
+
+    to_right = remote(bank.at[:, :, :, 1], own.at[0:frames, :, :, 0], near_sem.at[0], {"col": col + 1})
+    to_left = remote(bank.at[:, :, :, 0], own.at[0:frames, :, :, 3], near_sem.at[1], {"col": col - 1})
+    to_down = remote(bank.at[:, 1], rim.at[0:frames, 0, :, 1:3], row_sem.at[0], {"row": row + 1})
+    to_up = remote(bank.at[:, 0], rim.at[0:frames, 2, :, 1:3], row_sem.at[1], {"row": row - 1})
+    pl.when(right)(to_right.start)
+    pl.when(left)(to_left.start)
+    pl.when(down)(to_down.start)
+    pl.when(up)(to_up.start)
+
+    own[frames] = jnp.zeros_like(own[frames])
+    rim[frames] = jnp.zeros_like(rim[frames])
+
+    def clear(view, place):
+        for frame in range(frames):
+            view[(frame,) + place] = jnp.zeros_like(view[(frame,) + place])
+
+    every = slice(None)
+    pl.when(jnp.logical_not(up))(lambda: clear(rim, (0,)))
+    pl.when(jnp.logical_not(down))(lambda: clear(rim, (2,)))
+
+    @pl.when(jnp.logical_not(left))
+    def _():
+        clear(own, (every, every, 0))
+        clear(rim, (0, every, 0))
+        clear(rim, (2, every, 0))
+
+    @pl.when(jnp.logical_not(right))
+    def _():
+        clear(own, (every, every, 3))
+        clear(rim, (0, every, 3))
+        clear(rim, (2, every, 3))
+
+    centre.wait()
+    pl.when(left)(to_right.wait_recv)
+    pl.when(right)(to_left.wait_recv)
+
+    def decode(slot):
+        packed = served[slot]
+        shift_col = lax.rem(packed, 3) - 1
+        rest = lax.div(packed, 3)
+        return lax.div(rest, 3), lax.rem(rest, 3) - 1, shift_col
+
+    def pick(part, target, partner):
+        for spot in range(capacity):
+            slot = partner * capacity + spot
+            frame, shift_row, shift_col = decode(slot)
+            if part == 0:
+                line = jnp.where(shift_row < 0, 1, 0)
+                target[0, slot] = own[frame, line, :, pl.ds(1 - shift_col, 2)]
+            else:
+                target[1, slot] = rim[frame, 1 - shift_row, :, pl.ds(1 - shift_col, 2)]
+
+    sends = []
+
+    def send(part, step):
+        copy = remote(
+            chosen.at[part, pl.ds(partners[step - 1] * capacity, capacity)],
+            got.at[part, pl.ds(clip * capacity, capacity)],
+            clip_sem.at[part, step - 1],
+            {"clip": partners[step - 1]},
+        )
+        copy.start()
+        sends.append(copy)
+
+    for part in range(2):
+        if part == 1:
+            def keep(frame, carry):
+                rim[frame, 1] = own[frame, 1]
+                return carry
+
+            lax.fori_loop(0, frames, keep, 0)
+            pl.when(up)(to_down.wait_recv)
+            pl.when(down)(to_up.wait_recv)
+            corners = [
+                (up, right, remote(rim.at[0:frames, 0, :, 2], rim.at[0:frames, 0, :, 0], col_sem.at[0], {"col": col + 1})),
+                (down, right, remote(rim.at[0:frames, 2, :, 2], rim.at[0:frames, 2, :, 0], col_sem.at[1], {"col": col + 1})),
+                (up, left, remote(rim.at[0:frames, 0, :, 1], rim.at[0:frames, 0, :, 3], col_sem.at[2], {"col": col - 1})),
+                (down, left, remote(rim.at[0:frames, 2, :, 1], rim.at[0:frames, 2, :, 3], col_sem.at[3], {"col": col - 1})),
+            ]
+            for vertical, side, copy in corners:
+                pl.when(jnp.logical_and(vertical, side))(copy.start)
+            for (vertical, _, copy), other in zip(corners, (left, left, right, right)):
+                pl.when(jnp.logical_and(vertical, other))(copy.wait_recv)
+        for step in range(1, clips):
+            pick(part, chosen, partners[step - 1])
+            if step > 1:
+                send(part, step - 1)
+        pick(part, got, clip)
+        send(part, clips - 1)
+    for copy in sends:
+        copy.wait_recv()
+    slots = out.shape[0]
+    for slot in range(slots):
+        packed = wanted[slot]
+        place = lax.div(packed, 2)
+        flag = lax.rem(packed, 2)
+        out[slot, 0] = got[flag, place]
+        out[slot, 1] = got[1 - flag, place]
+    for copy in sends:
+        copy.wait_send()
+    pl.when(right)(to_right.wait_send)
+    pl.when(left)(to_left.wait_send)
+    pl.when(down)(to_down.wait_send)
+    pl.when(up)(to_up.wait_send)
+    for vertical, side, copy in corners:
+        pl.when(jnp.logical_and(vertical, side))(copy.wait_send)
+
+
+def fetch(bank, request, frame_pick, shift_rows, shift_cols, hist_count):
+    frames, height, width, channels = bank.shape
+    clips = lax.axis_size("clip")
+    capacity = (HIST + clips - 1) // clips
+    own_clip = lax.axis_index("clip")
+    slot_ids = own_clip * capacity + jnp.arange(capacity, dtype=jnp.int32)
+    matches = (request[:, None, :] == slot_ids[None, :, None]).astype(jnp.int32)
+    valid = jnp.arange(HIST)[None, :] < hist_count[:, None]
+    frame = jnp.where(valid, frame_pick, frames)
+    packed = (frame * 3 + shift_rows + 1) * 3 + shift_cols + 1
+    served = jnp.sum(matches * packed[:, None, :], axis=-1).reshape(-1)
+    pair = request * 2 + (shift_rows == 1).astype(jnp.int32)
+    wanted = lax.dynamic_index_in_dim(pair, own_clip, 0, False)
+    half = (height // 2, 2, width // 2, channels)
+    blocks = bank.reshape((frames, 2) + half)
+    wide = (height // 2, 4, width // 2, channels)
+    smem = pl.BlockSpec(memory_space=pltpu.SMEM)
+    dma = pltpu.SemaphoreType.DMA
+    out = pl.pallas_call(
+        fetch_kernel,
+        out_shape=jax.ShapeDtypeStruct((HIST, 2) + half, bank.dtype),
+        in_specs=[smem, smem, pl.BlockSpec(memory_space=pl.ANY)],
+        out_specs=pl.BlockSpec(memory_space=pltpu.VMEM),
+        scratch_shapes=[
+            pltpu.VMEM((frames + 1, 2) + wide, bank.dtype),
+            pltpu.VMEM((frames + 1, 3) + wide, bank.dtype),
+            pltpu.VMEM((2, clips * capacity) + half, bank.dtype),
+            pltpu.VMEM((2, clips * capacity) + half, bank.dtype),
+            dma((2, 2)),
+            dma((2, 2)),
+            dma((4, 2)),
+            dma((2, clips - 1, 2)),
+            dma,
+        ],
+        compiler_params=pltpu.CompilerParams(
+            collective_id=0, has_side_effects=True, vmem_limit_bytes=40 * 1024 * 1024
+        ),
+        name="fetch",
+    )(served, wanted, blocks)
+    return out.reshape(HIST, height * width, channels)
+
+
 def tap_views(padded, height, width, mirror):
     views = []
     for row_tap in range(3):
@@ -43,13 +239,6 @@
 def flipped(weight):
     channels = weight.shape[1]
     return weight.reshape(9, channels, channels).transpose(0, 2, 1).reshape(9 * channels, channels)
-
-
-def window_cut(padded, step_rows, step_cols, height, width, tile):
-    start_row = (1 - step_rows) * tile
-    start_col = (1 - step_cols) * tile
-    zero = jnp.int32(0)
-    return lax.dynamic_slice(padded, (start_row, start_col, zero), (height, width, padded.shape[2]))
 
 
 def local(
@@ -66,32 +255,9 @@
     grad_out,
 ):
     height, width, channels = (current.shape[1], current.shape[2], current.shape[3])
-    clip_count = lax.axis_size("clip")
-    capacity = (HIST + clip_count - 1) // clip_count
-    own_clip = lax.axis_index("clip")
-    slot_ids = own_clip * capacity + jnp.arange(capacity, dtype=jnp.int32)
-    matches = (request[:, None, :] == slot_ids[None, :, None]).astype(jnp.int32)
-    chosen = jnp.sum(matches * frame_pick[:, None, :], axis=-1).reshape(-1)
-    served = jnp.sum(matches, axis=-1).reshape(-1).astype(jnp.bfloat16)
-    own_request = lax.dynamic_index_in_dim(request, own_clip, 0, False)
-    own_rows = lax.dynamic_index_in_dim(shift_rows, own_clip, 0, False)
-    own_cols = lax.dynamic_index_in_dim(shift_cols, own_clip, 0, False)
-    own_count = lax.dynamic_index_in_dim(hist_count, own_clip, 0, False)
-    frames = bank[0]
-    outgoing = jnp.take(frames, chosen, axis=0) * served[:, None, None, None]
-    outgoing = outgoing.reshape(clip_count, capacity, height, width, channels)
-    received = lax.all_to_all(outgoing, "clip", split_axis=0, concat_axis=0, tiled=True)
-    fetched = jnp.take(
-        received.reshape(clip_count * capacity, height, width, channels), own_request, axis=0
-    )
-    padded_slots = extended(fetched, (("row", 1), ("col", 2)), TS)
-    warped = jax.vmap(
-        lambda slot, step_rows, step_cols: window_cut(slot, step_rows, step_cols, height, width, TS)
-    )(padded_slots, own_rows, own_cols)
-    valid = (jnp.arange(HIST) < own_count).astype(jnp.bfloat16)
-    warped = warped * valid[:, None, None, None]
+    warped = fetch(bank[0], request, frame_pick, shift_rows, shift_cols, hist_count)
     cells = height * width
-    stacked = jnp.concatenate([current[0][None], warped], axis=0).reshape(HIST + 1, cells, channels)
+    stacked = jnp.concatenate([current.reshape(1, cells, channels), warped], axis=0)
     join_blocks = join_weight.reshape(HIST + 1, channels, channels)
     joined = jnp.einsum(
         "kpc,kcd->pd", stacked, join_blocks, preferred_element_type=jnp.float32

time: 361 us -> 252 us (0.70)
  waiting for transfers between devices: 188 us -> 100 us
  Pallas kernels: 0 us -> 48.8 us
  local copies, waits for them, and re-layouts: 63.7 us -> 21.2 us
  other arithmetic: 27.1 us -> 13.4 us
  starting transfers between devices: 52.2 us -> 39.8 us
    pallas_call x0 -> x1, Pallas kernels: none -> 48.8 us  [fetch(): pl.pallas_call(fetch_kernel, out_shape=jax.ShapeDtypeStruct((HIST, 2) + h...]
    all_to_all x1 -> x0, waiting for transfers between devices: 48.2 us -> none  [local(): lax.all_to_all(outgoing, 'clip', split_axis=0, concat_axis=0, tiled=True)]
    ppermute x10 -> x8, waiting for transfers between devices: 25.7 us -> 0.02 us  [extended(): lax.ppermute(lax.slice_in_dim(block, 0, width, axis=dim), axis, backward)]
    ppermute x10 -> x8, waiting for transfers between devices: 19.7 us -> 0.02 us  [extended(): lax.ppermute(lax.slice_in_dim(block, block.shape[dim] - width, None, axis...]
    gather x3 -> x0, local copies, waits for them, and re-layouts: 14 us -> none  [the longest x1 7.14 us: window_cut(): lax.dynamic_slice(padded, (start_row, start_col, zero), (height, width, p...]
    concatenate x2 -> x0, local copies, waits for them, and re-layouts: 13.7 us -> none  [the longest x1 12.7 us: extended(): block = jnp.concatenate([low, block, high], axis=dim)]
    unnamed x70 -> x53, local copies, waits for them, and re-layouts: 22.3 us -> 15.5 us
    all_to_all x1 -> x0, starting transfers between devices: 6.48 us -> none  [local(): lax.all_to_all(outgoing, 'clip', split_axis=0, concat_axis=0, tiled=True)]
  transfers between devices with their start and end apart: 23 -> 18, of which waited for: 9 -> 2; matrix products, arithmetic and copies ran while one was open for 5% -> 6% of each run, Pallas kernels for 0% -> 0%
where the time goes in v2:
time: 252 us
  waiting for transfers between devices  100 us (40%)
  Pallas kernels  48.8 us (19%)
  starting transfers between devices  39.8 us (16%)
  local copies, waits for them, and re-layouts  21.2 us (8%)
  between operations  14.8 us (6%)
  other arithmetic  13.4 us (5%)
  matrix products  13.3 us (5%)
    reduce_scatter x1, waiting for transfers between devices, local(): lax.psum_scatter(shared, ('clip', 'row'), scatter_dimension=0, tiled=True)  81 us
    pallas_call x1, Pallas kernels, fetch(): pl.pallas_call(fetch_kernel, out_shape=jax.ShapeDtypeStruct((HIST, 2) + h...  48.8 us
    ppermute x8, starting transfers between devices, extended(): lax.ppermute(lax.slice_in_dim(block, block.shape[dim] - width, None, axis...  29.4 us
    unnamed x3, waiting for transfers between devices  19.2 us
    unnamed x53, local copies, waits for them, and re-layouts  15.5 us
    ppermute x8, starting transfers between devices, extended(): lax.ppermute(lax.slice_in_dim(block, 0, width, axis=dim), axis, backward)  10.3 us
    concatenate x1, other arithmetic, local(): term = jnp.concatenate([grad_join, grad_one, grad_two], axis=0)  7.03 us
    dot_general x1, matrix products, local(): jnp.einsum('kpc,pd->kcd', stacked, d_joined, preferred_element_type=jnp.f...  5.39 us
  transfers between devices with their start and end apart: 18, of which 2 were waited for; matrix products, arithmetic and copies ran while one was open for 6% of the time, Pallas kernels for 0%

profile of v2, /device:TPU:0, one launch (start us, length us, event | category | flops | bytes accessed | tf_op | source)
XLA Modules:
  0.0 251.5 jit_solution(5679063461784120204)
XLA Ops:
  7.2 0.9 convert_add_fusion
  8.2 0.9 select_reduce_fusion
  9.1 0.1 reshape.104.served
  9.2 1.2 copy-done.2
  10.4 48.8 %fetch.1 = bf16[15,2,8,2,8,256]{5,4,3,2,1,0:T(8,128)(2,1)S(1)} custom-call(s32[16]{0:T(128)S(1)} %reshape.104.served, s32[15]{0:T(128)S(1)} %dynamic-slice_bitcast_fusion.wanted, bf16[8,2,8,2,8,256]{5,4,3,2,1,0:T(8,128)(2,1)S(1)} %bitcast.95), custom_call_target="tpu_custom_call" | custom-call | tf_op jit(solution)/shard_map/fetch/pallas_call | solution.py:195
  59.3 1.4 broadcast_maximum_fusion
  60.7 0.6 slice_bitcast_fusion.5
  61.3 1.3 collective-permute-start.1
  62.6 5.1 %collective-permute-start = (bf16[1,16,256]{2,1,0:T(8,128)(2,1)}, bf16[1,16,256]{2,1,0:T(8,128)(2,1)}, u32[]{:S(2)}, u32[]{:S(2)}) collective-permute-start(bf16[1,16,256]{2,1,0:T(8,128)(2,1)} %get-tuple-element.56), channel_id=1, source_target_pairs={{0,2},{2,4},{4,6},{1,3},{3,5},{5,7},{8,10},{10,12},{12,14},{9,11},... | collective-permute-start | bytes 24584 | tf_op jit(solution)/shard_map/ppermute | solution.py:16
  67.7 0.6 slice_bitcast_fusion.7
  68.3 1.3 collective-permute-start.9
  69.6 4.7 %collective-permute-start.8 = (bf16[1,16,256]{2,1,0:T(8,128)(2,1)}, bf16[1,16,256]{2,1,0:T(8,128)(2,1)S(1)}, u32[]{:S(2)}, u32[]{:S(2)}) collective-permute-start(bf16[1,16,256]{2,1,0:T(8,128)(2,1)} %get-tuple-element.48), channel_id=1, source_target_pairs={{0,2},{2,4},{4,6},{1,3},{3,5},{5,7},{8,10},{10,12},{12,14},{9,11},... | collective-permute-start | bytes 24584 | tf_op jit(solution)/shard_map/ppermute | solution.py:16
  74.3 1.6 copy.21
  75.9 2.4 copy.22
  78.3 0.8 pad_maximum_fusion.29
  79.1 1.3 collective-permute-start.3
  80.4 3.0 %collective-permute-start.2 = (bf16[18,1,256]{2,1,0:T(2,128)(2,1)S(1)}, bf16[18,1,256]{2,1,0:T(2,128)(2,1)S(1)}, u32[]{:S(2)}, u32[]{:S(2)}) collective-permute-start(bf16[18,1,256]{2,1,0:T(2,128)(2,1)S(1)} %get-tuple-element.41), channel_id=1, source_target_pairs={{0,1},{2,3},{4,5},{6,7},{8,9},{10,11},{12,13},{14,15},{16,17},{18,... | collective-permute-start | bytes 27656 | tf_op jit(solution)/shard_map/ppermute | solution.py:16
  83.5 1.3 collective-permute-start.11
  84.8 1.3 collective-permute-start.10
  86.1 0.7 pad_maximum_fusion.18
  86.8 0.9 pad_maximum_fusion.8
  87.9 0.7 copy-done.7
  88.8 0.4 copy-done.4
  89.1 0.5 maximum_convert_fusion
  89.6 1.3 collective-permute-start.5
  90.9 5.4 %collective-permute-start.4 = (bf16[1,16,256]{2,1,0:T(8,128)(2,1)S(1)}, bf16[1,16,256]{2,1,0:T(8,128)(2,1)S(1)}, u32[]{:S(2)}, u32[]{:S(2)}) collective-permute-start(bf16[1,16,256]{2,1,0:T(8,128)(2,1)S(1)} %get-tuple-element.52), channel_id=1, source_target_pairs={{0,2},{2,4},{4,6},{1,3},{3,5},{5,7},{8,10},{10,12},{12,14},{9,11},... | collective-permute-start | bytes 24584 | tf_op jit(solution)/shard_map/ppermute | solution.py:16
  96.4 0.1 maximum_maximum_fusion.2
  96.8 1.1 copy-done.5
  97.9 0.5 fusion.4
  98.3 1.6 convolution_convert_fusion.1
  100.0 1.3 collective-permute-start.13
  101.3 5.4 %collective-permute-start.12 = (bf16[1,16,256]{2,1,0:T(8,128)(2,1)S(1)}, bf16[1,16,256]{2,1,0:T(8,128)(2,1)S(1)}, u32[]{:S(2)}, u32[]{:S(2)}) collective-permute-start(bf16[1,16,256]{2,1,0:T(8,128)(2,1)S(1)} %get-tuple-element.44), channel_id=1, source_target_pairs={{0,2},{2,4},{4,6},{1,3},{3,5},{5,7},{8,10},{10,12},{12,14},{9,11},... | collective-permute-start | bytes 24584 | tf_op jit(solution)/shard_map/ppermute | solution.py:16
  106.8 1.3 collective-permute-start.7
  108.1 3.0 %collective-permute-start.6 = (bf16[18,1,256]{2,1,0:T(2,128)(2,1)S(1)}, bf16[18,1,256]{2,1,0:T(2,128)(2,1)S(1)}, u32[]{:S(2)}, u32[]{:S(2)}) collective-permute-start(bf16[18,1,256]{2,1,0:T(2,128)(2,1)S(1)} %get-tuple-element.37), channel_id=1, source_target_pairs={{0,1},{2,3},{4,5},{6,7},{8,9},{10,11},{12,13},{14,15},{16,17},{18,... | collective-permute-start | bytes 27656 | tf_op jit(solution)/shard_map/ppermute | solution.py:16
  111.2 1.3 collective-permute-start.15
  112.5 1.3 collective-permute-start.14
  113.9 0.1 pad_maximum_fusion.9
  114.2 1.6 convolution_convert_fusion
  115.8 0.1 maximum_maximum_fusion.3
  116.2 1.0 copy-done.8
  117.2 5.4 %convolution_convert_fusion.2 = bf16[16,256,256]{2,1,0:T(8,128)(2,1)} fusion(bf16[15,256,256]{2,1,0:T(8,128)(2,1)} %bitcast.94, bf16[1,256,256]{2,1,0:T(8,128)(2,1)} %bitcast.151, bf16[256,2304]{1,0:T(8,128)(2,1)} %copy-done.8, bf16[2304,256]{1,0:T(8,128)(2,1)} %bitcast.117, bf16[256,256]{1,0:T(8,128)(2,1)S(1)} %bitcast.108, bf16[256,256]{1,0:T(8,128)(2,1)S(1)} %copy-done.7), kind=kOutput, calls=%fused_computation.4 | convolution fusion | flops 841285632 | bytes 6815744 | tf_op jit(solution)/shard_map/kpc,pd->kcd/dot_general | solution.py:292
  122.6 7.0 %pad_maximum_fusion = bf16[8704,256]{1,0:T(8,128)(2,1)} fusion(bf16[2304,256]{1,0:T(8,128)(2,1)} %convolution_convert_fusion, bf16[2304,256]{1,0:T(8,128)(2,1)} %convolution_convert_fusion.1, bf16[4096,256]{1,0:T(8,128)(2,1)} %bitcast.113), kind=kLoop, calls=%fused_computation | loop fusion | flops 13369344 | bytes 8912896 | tf_op jit(solution)/shard_map/concatenate | solution.py:295
  129.7 6.6 %copy.25 = bf16[8704,256]{0,1:T(8,128)(2,1)} copy(bf16[8704,256]{1,0:T(8,128)(2,1)} %pad_maximum_fusion) | data formatting | bytes 8912896
  136.3 19.2 %reduce-scatter.7.cloned.1.call-done = bf16[128,8704]{1,0:T(8,128)(2,1)} async-done(((bf16[256,8704]{1,0:T(8,128)(2,1)}), bf16[128,8704]{1,0:T(8,128)(2,1)}) %reduce-scatter.7.cloned.1.call-update) | async-done | bytes 2228240
  155.4 4.2 %copy.26 = bf16[8704,128]{1,0:T(8,128)(2,1)} copy(bf16[8704,128]{0,1:T(8,128)(2,1)} %bitcast.112) | data formatting | bytes 4456448
  159.6 2.4 fusion.3
  162.0 81.0 %reduce-scatter.5.cloned.1.call-done = bf16[544,128]{1,0:T(8,128)(2,1)} async-done(((bf16[8704,128]{1,0:T(8,128)(2,1)}), bf16[544,128]{1,0:T(8,128)(2,1)}) %reduce-scatter.5.cloned.1.call-update) | async-done | bytes 139280 | tf_op jit(solution)/shard_map/reduce_scatter | solution.py:299
  243.0 1.6 convert_element_type.37
  (87 shorter events, 1.1 us)
Async XLA Ops:
  7.2 52.1 %copy-start = (bf16[4096,256]{1,0:T(8,128)(2,1)S(1)}, bf16[4096,256]{1,0:T(8,128)(2,1)}, u32[]{:S(2)}) copy-start(bf16[4096,256]{1,0:T(8,128)(2,1)} %param.18) | copy-start | bytes 6291460
  7.2 148.3 %reduce-scatter.7.cloned.1.call-start = ((), (), s32[]{:S(2)}) async-start(), calls=%async_computation.3 | async-start | bytes 6684672
  9.2 1.2 copy-start.2
  10.4 48.9 %copy-start.9 = (bf16[1,16,16,256]{3,2,1,0:T(8,128)(2,1)S(1)}, bf16[1,16,16,256]{3,2,1,0:T(8,128)(2,1)}, u32[]{:S(2)}) copy-start(bf16[1,16,16,256]{3,2,1,0:T(8,128)(2,1)} %param.11) | copy-start | bytes 393220
  59.2 1.4 copy-start.1
  59.3 8.4 %copy-start.6 = (bf16[1,16,16,256]{3,2,1,0:T(8,128)(2,1)S(1)}, bf16[1,16,16,256]{3,2,1,0:T(8,128)(2,1)}, u32[]{:S(2)}) copy-start(bf16[1,16,16,256]{3,2,1,0:T(8,128)(2,1)} %param.21) | copy-start | bytes 393220
  59.3 15.0 %copy-start.3 = (bf16[2304,256]{1,0:T(8,128)(2,1)S(1)}, bf16[2304,256]{1,0:T(8,128)(2,1)}, u32[]{:S(2)}) copy-start(bf16[2304,256]{1,0:T(8,128)(2,1)} %param.20) | copy-start | bytes 3538948
  61.3 17.0 %collective-permute-start.1 = (bf16[1,16,256]{2,1,0:T(8,128)(2,1)}, bf16[1,16,256]{2,1,0:T(8,128)(2,1)}, u32[]{:S(2)}, u32[]{:S(2)}) collective-permute-start(bf16[1,16,256]{2,1,0:T(8,128)(2,1)} %get-tuple-element.57), channel_id=1, source_target_pairs={{2,0},{4,2},{6,4},{3,1},{5,3},{7,5},{10,8},{12,10},{14,12},{11,9},... | collective-permute-start | bytes 24584 | tf_op jit(solution)/shard_map/ppermute | solution.py:19
  62.6 15.7 %collective-permute-start = (bf16[1,16,256]{2,1,0:T(8,128)(2,1)}, bf16[1,16,256]{2,1,0:T(8,128)(2,1)}, u32[]{:S(2)}, u32[]{:S(2)}) collective-permute-start(bf16[1,16,256]{2,1,0:T(8,128)(2,1)} %get-tuple-element.56), channel_id=1, source_target_pairs={{0,2},{2,4},{4,6},{1,3},{3,5},{5,7},{8,10},{10,12},{12,14},{9,11},... | collective-permute-start | bytes 24584 | tf_op jit(solution)/shard_map/ppermute | solution.py:16
  68.3 15.1 %collective-permute-start.9 = (bf16[1,16,256]{2,1,0:T(8,128)(2,1)}, bf16[1,16,256]{2,1,0:T(8,128)(2,1)S(1)}, u32[]{:S(2)}, u32[]{:S(2)}) collective-permute-start(bf16[1,16,256]{2,1,0:T(8,128)(2,1)} %get-tuple-element.49), channel_id=1, source_target_pairs={{2,0},{4,2},{6,4},{3,1},{5,3},{7,5},{10,8},{12,10},{14,12},{11,9},... | collective-permute-start | bytes 24584 | tf_op jit(solution)/shard_map/ppermute | solution.py:19
  69.6 13.8 %collective-permute-start.8 = (bf16[1,16,256]{2,1,0:T(8,128)(2,1)}, bf16[1,16,256]{2,1,0:T(8,128)(2,1)S(1)}, u32[]{:S(2)}, u32[]{:S(2)}) collective-permute-start(bf16[1,16,256]{2,1,0:T(8,128)(2,1)} %get-tuple-element.48), channel_id=1, source_target_pairs={{0,2},{2,4},{4,6},{1,3},{3,5},{5,7},{8,10},{10,12},{12,14},{9,11},... | collective-permute-start | bytes 24584 | tf_op jit(solution)/shard_map/ppermute | solution.py:16
  79.1 7.8 %collective-permute-start.3 = (bf16[18,1,256]{2,1,0:T(2,128)(2,1)S(1)}, bf16[18,1,256]{2,1,0:T(2,128)(2,1)S(1)}, u32[]{:S(2)}, u32[]{:S(2)}) collective-permute-start(bf16[18,1,256]{2,1,0:T(2,128)(2,1)S(1)} %get-tuple-element.40), channel_id=1, source_target_pairs={{1,0},{3,2},{5,4},{7,6},{9,8},{11,10},{13,12},{15,14},{17,16},{19,... | collective-permute-start | bytes 27656 | tf_op jit(solution)/shard_map/ppermute | solution.py:19
  80.4 6.5 %collective-permute-start.2 = (bf16[18,1,256]{2,1,0:T(2,128)(2,1)S(1)}, bf16[18,1,256]{2,1,0:T(2,128)(2,1)S(1)}, u32[]{:S(2)}, u32[]{:S(2)}) collective-permute-start(bf16[18,1,256]{2,1,0:T(2,128)(2,1)S(1)} %get-tuple-element.41), channel_id=1, source_target_pairs={{0,1},{2,3},{4,5},{6,7},{8,9},{10,11},{12,13},{14,15},{16,17},{18,... | collective-permute-start | bytes 27656 | tf_op jit(solution)/shard_map/ppermute | solution.py:16
  83.5 12.9 %collective-permute-start.11 = (bf16[18,1,256]{2,1,0:T(2,128)(2,1)S(1)}, bf16[18,1,256]{2,1,0:T(2,128)(2,1)S(1)}, u32[]{:S(2)}, u32[]{:S(2)}) collective-permute-start(bf16[18,1,256]{2,1,0:T(2,128)(2,1)S(1)} %get-tuple-element.32), channel_id=1, source_target_pairs={{0,1},{2,3},{4,5},{6,7},{8,9},{10,11},{12,13},{14,15},{16,17},{18,... | collective-permute-start | bytes 27656 | tf_op jit(solution)/shard_map/ppermute | solution.py:16
  84.8 11.6 %collective-permute-start.10 = (bf16[18,1,256]{2,1,0:T(2,128)(2,1)S(1)}, bf16[18,1,256]{2,1,0:T(2,128)(2,1)S(1)}, u32[]{:S(2)}, u32[]{:S(2)}) collective-permute-start(bf16[18,1,256]{2,1,0:T(2,128)(2,1)S(1)} %get-tuple-element.33), channel_id=1, source_target_pairs={{1,0},{3,2},{5,4},{7,6},{9,8},{11,10},{13,12},{15,14},{17,16},{19,... | collective-permute-start | bytes 27656 | tf_op jit(solution)/shard_map/ppermute | solution.py:19
  87.7 0.9 copy-start.7
  87.8 1.3 copy-start.4
  89.6 17.1 %collective-permute-start.5 = (bf16[1,16,256]{2,1,0:T(8,128)(2,1)S(1)}, bf16[1,16,256]{2,1,0:T(8,128)(2,1)S(1)}, u32[]{:S(2)}, u32[]{:S(2)}) collective-permute-start(bf16[1,16,256]{2,1,0:T(8,128)(2,1)S(1)} %get-tuple-element.53), channel_id=1, source_target_pairs={{2,0},{4,2},{6,4},{3,1},{5,3},{7,5},{10,8},{12,10},{14,12},{11,9},... | collective-permute-start | bytes 24584 | tf_op jit(solution)/shard_map/ppermute | solution.py:19
  90.9 15.8 %collective-permute-start.4 = (bf16[1,16,256]{2,1,0:T(8,128)(2,1)S(1)}, bf16[1,16,256]{2,1,0:T(8,128)(2,1)S(1)}, u32[]{:S(2)}, u32[]{:S(2)}) collective-permute-start(bf16[1,16,256]{2,1,0:T(8,128)(2,1)S(1)} %get-tuple-element.52), channel_id=1, source_target_pairs={{0,2},{2,4},{4,6},{1,3},{3,5},{5,7},{8,10},{10,12},{12,14},{9,11},... | collective-permute-start | bytes 24584 | tf_op jit(solution)/shard_map/ppermute | solution.py:16
  96.6 1.3 copy-start.5
  100.0 11.1 %collective-permute-start.13 = (bf16[1,16,256]{2,1,0:T(8,128)(2,1)S(1)}, bf16[1,16,256]{2,1,0:T(8,128)(2,1)S(1)}, u32[]{:S(2)}, u32[]{:S(2)}) collective-permute-start(bf16[1,16,256]{2,1,0:T(8,128)(2,1)S(1)} %get-tuple-element.45), channel_id=1, source_target_pairs={{2,0},{4,2},{6,4},{3,1},{5,3},{7,5},{10,8},{12,10},{14,12},{11,9},... | collective-permute-start | bytes 24584 | tf_op jit(solution)/shard_map/ppermute | solution.py:19
  101.3 9.9 %collective-permute-start.12 = (bf16[1,16,256]{2,1,0:T(8,128)(2,1)S(1)}, bf16[1,16,256]{2,1,0:T(8,128)(2,1)S(1)}, u32[]{:S(2)}, u32[]{:S(2)}) collective-permute-start(bf16[1,16,256]{2,1,0:T(8,128)(2,1)S(1)} %get-tuple-element.44), channel_id=1, source_target_pairs={{0,2},{2,4},{4,6},{1,3},{3,5},{5,7},{8,10},{10,12},{12,14},{9,11},... | collective-permute-start | bytes 24584 | tf_op jit(solution)/shard_map/ppermute | solution.py:16
  106.8 7.1 %collective-permute-start.7 = (bf16[18,1,256]{2,1,0:T(2,128)(2,1)S(1)}, bf16[18,1,256]{2,1,0:T(2,128)(2,1)S(1)}, u32[]{:S(2)}, u32[]{:S(2)}) collective-permute-start(bf16[18,1,256]{2,1,0:T(2,128)(2,1)S(1)} %get-tuple-element.36), channel_id=1, source_target_pairs={{1,0},{3,2},{5,4},{7,6},{9,8},{11,10},{13,12},{15,14},{17,16},{19,... | collective-permute-start | bytes 27656 | tf_op jit(solution)/shard_map/ppermute | solution.py:19
  108.1 5.8 %collective-permute-start.6 = (bf16[18,1,256]{2,1,0:T(2,128)(2,1)S(1)}, bf16[18,1,256]{2,1,0:T(2,128)(2,1)S(1)}, u32[]{:S(2)}, u32[]{:S(2)}) collective-permute-start(bf16[18,1,256]{2,1,0:T(2,128)(2,1)S(1)} %get-tuple-element.37), channel_id=1, source_target_pairs={{0,1},{2,3},{4,5},{6,7},{8,9},{10,11},{12,13},{14,15},{16,17},{18,... | collective-permute-start | bytes 27656 | tf_op jit(solution)/shard_map/ppermute | solution.py:16
  111.2 4.6 %collective-permute-start.15 = (bf16[18,1,256]{2,1,0:T(2,128)(2,1)S(1)}, bf16[18,1,256]{2,1,0:T(2,128)(2,1)S(1)}, u32[]{:S(2)}, u32[]{:S(2)}) collective-permute-start(bf16[18,1,256]{2,1,0:T(2,128)(2,1)S(1)} %get-tuple-element.28), channel_id=1, source_target_pairs={{0,1},{2,3},{4,5},{6,7},{8,9},{10,11},{12,13},{14,15},{16,17},{18,... | collective-permute-start | bytes 27656 | tf_op jit(solution)/shard_map/ppermute | solution.py:16
  112.5 3.3 %collective-permute-start.14 = (bf16[18,1,256]{2,1,0:T(2,128)(2,1)S(1)}, bf16[18,1,256]{2,1,0:T(2,128)(2,1)S(1)}, u32[]{:S(2)}, u32[]{:S(2)}) collective-permute-start(bf16[18,1,256]{2,1,0:T(2,128)(2,1)S(1)} %get-tuple-element.29), channel_id=1, source_target_pairs={{1,0},{3,2},{5,4},{7,6},{9,8},{11,10},{13,12},{15,14},{17,16},{19,... | collective-permute-start | bytes 27656 | tf_op jit(solution)/shard_map/ppermute | solution.py:19
  116.2 1.0 copy-start.8
  136.2 106.8 %reduce-scatter.5.cloned.1.call-start = ((), (), s32[]{:S(2)}) async-start(), calls=%async_computation.2 | async-start | bytes 2367488 | tf_op jit(solution)/shard_map/reduce_scatter | solution.py:299
Sparse Core Ops, SparseCore 0:
  136.3 19.0 reduce-scatter.6
  159.8 83.2 reduce-scatter.4

commit v3 on v2

--- a/solution.py
+++ b/solution.py
@@ -223,7 +223,7 @@
             top = 2 - row_tap if mirror else row_tap
             left = 2 - col_tap if mirror else col_tap
             views.append(padded[top : top + height, left : left + width])
-    return jnp.concatenate(views, axis=-1).reshape(height * width, -1)
+    return jnp.stack(views).reshape(9, height * width, -1)
 
 
 def forward_patch(field):
@@ -238,7 +238,179 @@
 
 def flipped(weight):
     channels = weight.shape[1]
-    return weight.reshape(9, channels, channels).transpose(0, 2, 1).reshape(9 * channels, channels)
+    return weight.reshape(9, channels, channels).transpose(0, 2, 1)
+
+
+def flip(index, bit):
+    return index + bit - 2 * bit * lax.rem(lax.div(index, bit), 2)
+
+
+def gradient_kernel(
+    counts, lhs, rhs, out, term, near_out, near_in, far_out, far_in, last_out, last_in, clip_out, clip_in,
+    near_sem, far_sem, last_sem, clip_sem
+):
+    clips = lax.axis_size("clip")
+    rows = lax.axis_size("row")
+    clip = lax.axis_index("clip")
+    row = lax.axis_index("row")
+    col = lax.axis_index("col")
+    bits = (1, 2)
+    peers = [{"col": 1 - col}] + [{"row": flip(row, bit)} for bit in bits]
+    peers += [{"clip": lax.rem(clip + step, clips)} for step in range(1, clips)]
+    for where in peers:
+        pl.semaphore_signal(
+            pltpu.get_barrier_semaphore(), inc=1, device_id=where, device_id_type=pl.DeviceIdType.MESH
+        )
+    pl.semaphore_wait(pltpu.get_barrier_semaphore(), len(peers))
+
+    def remote(source, target, sems, where):
+        return pltpu.make_async_remote_copy(
+            src_ref=source,
+            dst_ref=target,
+            send_sem=sems.at[0],
+            recv_sem=sems.at[1],
+            device_id=where,
+            device_id_type=pl.DeviceIdType.MESH,
+        )
+
+    size = lhs.shape[2]
+    lanes = term.shape[4]
+    part_rows = term.shape[3]
+    index = 0
+    for group, count in enumerate(counts):
+        for _ in range(count):
+            product = lax.dot_general(
+                lhs[index], rhs[group], (((0,), (0,)), ((), ())), preferred_element_type=jnp.float32
+            )
+            start = index * size
+            done = 0
+            while done < size:
+                place = start + done
+                piece = place // part_rows
+                inside = place % part_rows
+                length = min(size - done, part_rows - inside)
+                for side in range(2):
+                    term[side, piece // 2, piece % 2, inside : inside + length] = product[
+                        done : done + length, side * lanes : (side + 1) * lanes
+                    ]
+                done += length
+            index += 1
+
+    order = [lax.rem(clip + step, clips) for step in range(1, clips)] + [clip]
+    near = []
+    for turn, target in enumerate(order):
+        for spot in range(rows):
+            block = target * rows + spot
+            near_out[block] = term[1 - col, block].astype(near_out.dtype)
+        near.append(
+            remote(
+                near_out.at[pl.ds(target * rows, rows)],
+                near_in.at[pl.ds(target * rows, rows)],
+                near_sem.at[turn],
+                {"col": 1 - col},
+            )
+        )
+        near[-1].start()
+
+    def near_sum(turn, part, offset):
+        spot = row
+        for bit in bits:
+            if offset & bit:
+                spot = flip(spot, bit)
+        block = order[turn] * rows + spot
+        return term[col, block, part] + near_in[block, part].astype(jnp.float32)
+
+    far, last, final = {}, {}, []
+
+    def first(turn):
+        near[turn].wait_recv()
+        for part in range(2):
+            one, two = bits if part == 0 else bits[::-1]
+            for spot, offset in enumerate((one, one + two)):
+                far_out[turn, part, spot] = near_sum(turn, part, offset).astype(far_out.dtype)
+            far[turn, part] = remote(
+                far_out.at[turn, part], far_in.at[turn, part], far_sem.at[turn, part], {"row": flip(row, one)}
+            )
+            far[turn, part].start()
+
+    def second(turn):
+        for part in range(2):
+            one, two = bits if part == 0 else bits[::-1]
+            far[turn, part].wait_recv()
+            total = near_sum(turn, part, two) + far_in[turn, part, 1].astype(jnp.float32)
+            last_out[turn, part] = total.astype(last_out.dtype)
+            last[turn, part] = remote(
+                last_out.at[turn, part], last_in.at[turn, part], last_sem.at[turn, part], {"row": flip(row, two)}
+            )
+            last[turn, part].start()
+
+    def third(turn):
+        for part in range(2):
+            last[turn, part].wait_recv()
+            total = near_sum(turn, part, 0) + far_in[turn, part, 0].astype(jnp.float32)
+            total = total + last_in[turn, part].astype(jnp.float32)
+            if turn < clips - 1:
+                clip_out[turn, part] = total.astype(clip_out.dtype)
+            else:
+                out[part] = total
+        if turn < clips - 1:
+            copy = remote(clip_out.at[turn], clip_in.at[turn], clip_sem.at[turn], {"clip": order[turn]})
+            copy.start()
+            final.append(copy)
+
+    for turn in range(clips + 2):
+        if turn < clips:
+            first(turn)
+        if 0 <= turn - 1 < clips:
+            second(turn - 1)
+        if turn >= 2:
+            third(turn - 2)
+    for turn, copy in enumerate(final):
+        copy.wait_recv()
+        for part in range(2):
+            out[part] += clip_in[turn, part].astype(jnp.float32)
+    for copy in near + list(far.values()) + list(last.values()) + final:
+        copy.wait_send()
+
+
+def gradients(groups):
+    lhs = jnp.concatenate([group[0] for group in groups], axis=0)
+    rhs = jnp.stack([group[1] for group in groups])
+    counts = tuple(group[0].shape[0] for group in groups)
+    clips = lax.axis_size("clip")
+    rows = lax.axis_size("row")
+    total = lhs.shape[0] * lhs.shape[2]
+    part_rows = total // (2 * clips * rows)
+    lanes = rhs.shape[2] // lax.axis_size("col")
+    piece = (part_rows, lanes)
+    vmem = pl.BlockSpec(memory_space=pltpu.VMEM)
+    dma = pltpu.SemaphoreType.DMA
+    out = pl.pallas_call(
+        lambda *refs: gradient_kernel(counts, *refs),
+        out_shape=jax.ShapeDtypeStruct((2,) + piece, jnp.float32),
+        in_specs=[vmem, vmem],
+        out_specs=vmem,
+        scratch_shapes=[
+            pltpu.VMEM((2, clips * rows, 2) + piece, jnp.float32),
+            pltpu.VMEM((clips * rows, 2) + piece, jnp.bfloat16),
+            pltpu.VMEM((clips * rows, 2) + piece, jnp.bfloat16),
+            pltpu.VMEM((clips, 2, rows // 2) + piece, jnp.bfloat16),
+            pltpu.VMEM((clips, 2, rows // 2) + piece, jnp.bfloat16),
+            pltpu.VMEM((clips, 2) + piece, jnp.bfloat16),
+            pltpu.VMEM((clips, 2) + piece, jnp.bfloat16),
+            pltpu.VMEM((clips - 1, 2) + piece, jnp.bfloat16),
+            pltpu.VMEM((clips - 1, 2) + piece, jnp.bfloat16),
+            dma((clips, 2)),
+            dma((clips, 2, 2)),
+            dma((clips, 2, 2)),
+            dma((clips - 1, 2)),
+        ],
+        compiler_params=pltpu.CompilerParams(
+            collective_id=1, has_side_effects=True, vmem_limit_bytes=48 * 1024 * 1024
+        ),
+        name="gradients",
+    )(lhs, rhs)
+    return out.reshape(2 * part_rows, lanes)
 
 
 def local(
@@ -264,10 +436,10 @@
     ).astype(jnp.bfloat16)
     act = jnp.maximum(joined, 0)
     act_patch = forward_patch(act.reshape(height, width, channels))
-    conv1 = jnp.dot(act_patch, conv_one, preferred_element_type=jnp.float32)
+    conv1 = jnp.einsum("tpc,tcd->pd", act_patch, conv_one.reshape(9, channels, channels), preferred_element_type=jnp.float32)
     hidden = jnp.maximum(conv1, 0.0).astype(jnp.bfloat16)
     hidden_patch = forward_patch(hidden.reshape(height, width, channels))
-    conv2 = jnp.dot(hidden_patch, conv_two, preferred_element_type=jnp.float32)
+    conv2 = jnp.einsum("tpc,tcd->pd", hidden_patch, conv_two.reshape(9, channels, channels), preferred_element_type=jnp.float32)
     encoded = (
         (joined.astype(jnp.float32) + conv2)
         .astype(jnp.bfloat16)
@@ -275,13 +447,12 @@
     )
     upstream = grad_out[0]
     flat_up = upstream.reshape(cells, channels)
-    grad_two = jnp.dot(hidden_patch.T, flat_up, preferred_element_type=jnp.float32)
-    d_hidden = jnp.dot(
-        backward_patch(upstream), flipped(conv_two), preferred_element_type=jnp.float32
+    d_hidden = jnp.einsum(
+        "tpc,tcd->pd", backward_patch(upstream), flipped(conv_two), preferred_element_type=jnp.float32
     )
     d_conv1 = jnp.where(conv1 > 0, d_hidden, 0.0).astype(jnp.bfloat16)
-    grad_one = jnp.dot(act_patch.T, d_conv1, preferred_element_type=jnp.float32)
-    d_act = jnp.dot(
+    d_act = jnp.einsum(
+        "tpc,tcd->pd",
         backward_patch(d_conv1.reshape(height, width, channels)),
         flipped(conv_one),
         preferred_element_type=jnp.float32,
@@ -289,16 +460,9 @@
     d_joined = (flat_up.astype(jnp.float32) + jnp.where(joined > 0, d_act, 0.0)).astype(
         jnp.bfloat16
     )
-    grad_join = jnp.einsum(
-        "kpc,pd->kcd", stacked, d_joined, preferred_element_type=jnp.float32
-    ).reshape((HIST + 1) * channels, channels)
-    term = jnp.concatenate([grad_join, grad_one, grad_two], axis=0)
-    shared = lax.psum_scatter(
-        term.astype(jnp.bfloat16), "col", scatter_dimension=1, tiled=True
-    )
-    weight_grads = lax.psum_scatter(
-        shared, ("clip", "row"), scatter_dimension=0, tiled=True
-    ).astype(jnp.float32)
+    weight_grads = gradients(
+        ((stacked, d_joined), (act_patch, d_conv1), (hidden_patch, flat_up))
+    )
     return (encoded, weight_grads)
 
 

time: 252 us -> 155 us (0.62)
  waiting for transfers between devices: 100 us -> 0.13 us
  Pallas kernels: 48.8 us -> 85.9 us
  between operations: 14.8 us -> 1.36 us
  matrix products: 13.3 us -> 3.94 us
  other arithmetic: 13.4 us -> 5.43 us
  local copies, waits for them, and re-layouts: 21.2 us -> 17.7 us
    reduce_scatter x1 -> x0, waiting for transfers between devices: 81 us -> none  [local(): lax.psum_scatter(shared, ('clip', 'row'), scatter_dimension=0, tiled=True)]
    pallas_call x0 -> x1, Pallas kernels: none -> 37.1 us  [gradients(): pl.pallas_call(lambda *refs: gradient_kernel(counts, *refs), out_shape=ja...]
    unnamed x3 -> x0, waiting for transfers between devices: 19.2 us -> none
    dot_general x6 -> x4, matrix products: 11.9 us -> 2.57 us  [the longest x1 1.14 us: local(): jnp.einsum('tpc,tcd->pd', hidden_patch, conv_two.reshape(9, channels, cha...]
    concatenate x1 -> x0, other arithmetic: 7.03 us -> none  [local(): term = jnp.concatenate([grad_join, grad_one, grad_two], axis=0)]
    transpose x2 -> x0, local copies, waits for them, and re-layouts: 3.96 us -> none  [flipped(): weight.reshape(9, channels, channels).transpose(0, 2, 1)]
    reshape x0 -> x2, local copies, waits for them, and re-layouts: none -> 3.9 us  [the longest x1 2.37 us: local(): conv_one.reshape(9, channels, channels)]
    unnamed x53 -> x57, local copies, waits for them, and re-layouts: 15.5 us -> 12.1 us
  transfers between devices with their start and end apart: 18 -> 16, of which waited for: 2 -> 1; matrix products, arithmetic and copies ran while one was open for 6% -> 10% of each run, Pallas kernels for 0% -> 0%
where the time goes in v3:
time: 155 us; the launch traced here: 154 us
  Pallas kernels  85.9 us (55%)
  starting transfers between devices  40 us (26%)
  local copies, waits for them, and re-layouts  17.7 us (11%)
  other arithmetic  5.43 us (4%)
  matrix products  3.94 us (3%)
    pallas_call x1, Pallas kernels, fetch(): pl.pallas_call(fetch_kernel, out_shape=jax.ShapeDtypeStruct((HIST, 2) + h...  48.8 us
    pallas_call x1, Pallas kernels, gradients(): pl.pallas_call(lambda *refs: gradient_kernel(counts, *refs), out_shape=ja...  37.1 us
    ppermute x8, starting transfers between devices, extended(): lax.ppermute(lax.slice_in_dim(block, block.shape[dim] - width, None, axis...  29.4 us
    unnamed x57, local copies, waits for them, and re-layouts  12.1 us
    ppermute x8, starting transfers between devices, extended(): lax.ppermute(lax.slice_in_dim(block, 0, width, axis=dim), axis, backward)  10.6 us
  transfers between devices with their start and end apart: 16, of which 1 were waited for; matrix products, arithmetic and copies ran while one was open for 10% of the time, Pallas kernels for 0%

profile of v3, /device:TPU:0, one launch (start us, length us, event | category | flops | bytes accessed | tf_op | source)
XLA Modules:
  0.0 154.4 jit_solution(1344726697694998008)
XLA Ops:
  0.7 1.0 convert_add_fusion
  1.6 0.9 select_reduce_fusion
  2.6 1.2 copy-done.3
  3.8 48.8 %fetch.1 = bf16[15,2,8,2,8,256]{5,4,3,2,1,0:T(8,128)(2,1)S(1)} custom-call(s32[16]{0:T(128)S(1)} %reshape.132.served, s32[15]{0:T(128)S(1)} %dynamic-slice_bitcast_fusion.wanted, bf16[8,2,8,2,8,256]{5,4,3,2,1,0:T(8,128)(2,1)S(1)} %bitcast.216), custom_call_target="tpu_custom_call" | custom-call | tf_op jit(solution)/shard_map/fetch/pallas_call | solution.py:195
  52.7 1.4 broadcast_maximum_fusion
  54.1 0.6 slice_bitcast_fusion.5
  54.7 1.3 collective-permute-start.1
  56.0 5.1 %collective-permute-start = (bf16[1,16,256]{2,1,0:T(8,128)(2,1)}, bf16[1,16,256]{2,1,0:T(8,128)(2,1)}, u32[]{:S(2)}, u32[]{:S(2)}) collective-permute-start(bf16[1,16,256]{2,1,0:T(8,128)(2,1)} %get-tuple-element.92), channel_id=1, source_target_pairs={{0,2},{2,4},{4,6},{1,3},{3,5},{5,7},{8,10},{10,12},{12,14},{9,11},... | collective-permute-start | bytes 24584 | tf_op jit(solution)/shard_map/ppermute | solution.py:16
  61.1 0.6 slice_bitcast_fusion.7
  61.7 1.3 collective-permute-start.9
  63.0 4.7 %collective-permute-start.8 = (bf16[1,16,256]{2,1,0:T(8,128)(2,1)}, bf16[1,16,256]{2,1,0:T(8,128)(2,1)S(1)}, u32[]{:S(2)}, u32[]{:S(2)}) collective-permute-start(bf16[1,16,256]{2,1,0:T(8,128)(2,1)} %get-tuple-element.48), channel_id=1, source_target_pairs={{0,2},{2,4},{4,6},{1,3},{3,5},{5,7},{8,10},{10,12},{12,14},{9,11},... | collective-permute-start | bytes 24584 | tf_op jit(solution)/shard_map/ppermute | solution.py:16
  67.8 0.2 constant_dynamic-update-slice_fusion
  68.0 2.1 %copy-done.1 = bf16[34,256,256]{2,1,0:T(8,128)(2,1)} copy-done((bf16[34,256,256]{2,1,0:T(8,128)(2,1)}, bf16[34,256,256]{2,1,0:T(8,128)(2,1)S(1)}, u32[]{:S(2)}) %copy-start.1) | copy-done | bytes 4456472
  70.0 1.5 copy.15
  71.6 2.4 %copy.16 = bf16[9,256,256]{1,2,0:T(8,128)(2,1)} copy(bf16[9,256,256]{2,1,0:T(8,128)(2,1)} %bitcast.223) | data formatting | bytes 2359296 | tf_op jit(solution)/shard_map/reshape | solution.py:439
  73.9 0.7 pad_maximum_fusion.22
  74.7 1.3 collective-permute-start.3
  76.0 3.0 %collective-permute-start.2 = (bf16[18,1,256]{2,1,0:T(2,128)(2,1)S(1)}, bf16[18,1,256]{2,1,0:T(2,128)(2,1)S(1)}, u32[]{:S(2)}, u32[]{:S(2)}) collective-permute-start(bf16[18,1,256]{2,1,0:T(2,128)(2,1)S(1)} %get-tuple-element.41), channel_id=1, source_target_pairs={{0,1},{2,3},{4,5},{6,7},{8,9},{10,11},{12,13},{14,15},{16,17},{18,... | collective-permute-start | bytes 27656 | tf_op jit(solution)/shard_map/ppermute | solution.py:16
  79.1 1.3 collective-permute-start.11
  80.4 1.3 collective-permute-start.10
  81.7 0.7 pad_maximum_fusion.11
  82.5 0.9 pad_maximum_fusion.1
  83.4 0.7 bitcast_dynamic-update-slice_fusion.50
  84.1 0.7 bitcast_dynamic-update-slice_fusion.48
  84.7 0.7 bitcast_dynamic-update-slice_fusion.46
  85.4 0.7 bitcast_dynamic-update-slice_fusion.44
  86.1 0.7 bitcast_dynamic-update-slice_fusion.42
  86.8 0.7 bitcast_dynamic-update-slice_fusion.40
  87.4 0.7 bitcast_dynamic-update-slice_fusion.38
  88.1 0.7 bitcast_dynamic-update-slice_fusion.36
  88.8 0.7 bitcast_dynamic-update-slice_fusion.34
  89.5 0.5 maximum_convert_fusion
  90.0 1.3 collective-permute-start.5
  91.3 5.4 %collective-permute-start.4 = (bf16[1,16,256]{2,1,0:T(8,128)(2,1)S(1)}, bf16[1,16,256]{2,1,0:T(8,128)(2,1)S(1)}, u32[]{:S(2)}, u32[]{:S(2)}) collective-permute-start(bf16[1,16,256]{2,1,0:T(8,128)(2,1)S(1)} %get-tuple-element.88), channel_id=1, source_target_pairs={{0,2},{2,4},{4,6},{1,3},{3,5},{5,7},{8,10},{10,12},{12,14},{9,11},... | collective-permute-start | bytes 24584 | tf_op jit(solution)/shard_map/ppermute | solution.py:16
  96.7 0.1 maximum_maximum_fusion.2
  97.1 1.1 copy-done.6
  98.2 0.5 fusion.27
  98.7 1.6 %collective-permute-start.13 = (bf16[1,16,256]{2,1,0:T(8,128)(2,1)S(1)}, bf16[1,16,256]{2,1,0:T(8,128)(2,1)S(1)}, u32[]{:S(2)}, u32[]{:S(2)}) collective-permute-start(bf16[1,16,256]{2,1,0:T(8,128)(2,1)S(1)} %get-tuple-element.45), channel_id=1, source_target_pairs={{2,0},{4,2},{6,4},{3,1},{5,3},{7,5},{10,8},{12,10},{14,12},{11,9},... | collective-permute-start | bytes 24584 | tf_op jit(solution)/shard_map/ppermute | solution.py:19
  100.3 5.4 %collective-permute-start.12 = (bf16[1,16,256]{2,1,0:T(8,128)(2,1)S(1)}, bf16[1,16,256]{2,1,0:T(8,128)(2,1)S(1)}, u32[]{:S(2)}, u32[]{:S(2)}) collective-permute-start(bf16[1,16,256]{2,1,0:T(8,128)(2,1)S(1)} %get-tuple-element.44), channel_id=1, source_target_pairs={{0,2},{2,4},{4,6},{1,3},{3,5},{5,7},{8,10},{10,12},{12,14},{9,11},... | collective-permute-start | bytes 24584 | tf_op jit(solution)/shard_map/ppermute | solution.py:16
  105.8 1.3 collective-permute-start.7
  107.1 3.0 %collective-permute-start.6 = (bf16[18,1,256]{2,1,0:T(2,128)(2,1)S(1)}, bf16[18,1,256]{2,1,0:T(2,128)(2,1)S(1)}, u32[]{:S(2)}, u32[]{:S(2)}) collective-permute-start(bf16[18,1,256]{2,1,0:T(2,128)(2,1)S(1)} %get-tuple-element.37), channel_id=1, source_target_pairs={{0,1},{2,3},{4,5},{6,7},{8,9},{10,11},{12,13},{14,15},{16,17},{18,... | collective-permute-start | bytes 27656 | tf_op jit(solution)/shard_map/ppermute | solution.py:16
  110.2 1.3 collective-permute-start.15
  111.5 1.3 collective-permute-start.14
  113.3 1.1 fusion.33
  115.0 1.1 copy-done.8
  116.1 0.5 fusion.37
  116.6 37.1 %gradients.1 = f32[2,272,128]{2,1,0:T(8,128)S(1)} custom-call(bf16[34,256,256]{2,1,0:T(8,128)(2,1)S(1)} %get-tuple-element.50.refs_0_, bf16[3,256,256]{2,1,0:T(8,128)(2,1)S(1)} %pad_maximum_fusion.refs_1_), custom_call_target="tpu_custom_call" | custom-call | tf_op jit(solution)/shard_map/gradients/pallas_call | solution.py:388
  153.7 0.7 copy.69
  (82 shorter events, 1.4 us)
Async XLA Ops:
  0.6 52.0 %copy-start = (bf16[4096,256]{1,0:T(8,128)(2,1)S(1)}, bf16[4096,256]{1,0:T(8,128)(2,1)}, u32[]{:S(2)}) copy-start(bf16[4096,256]{1,0:T(8,128)(2,1)} %param.18) | copy-start | bytes 6291460
  2.6 1.2 copy-start.3
  3.8 48.8 %copy-start.10 = (bf16[1,16,16,256]{3,2,1,0:T(8,128)(2,1)S(1)}, bf16[1,16,16,256]{3,2,1,0:T(8,128)(2,1)}, u32[]{:S(2)}) copy-start(bf16[1,16,16,256]{3,2,1,0:T(8,128)(2,1)} %param.11) | copy-start | bytes 393220
  52.7 8.4 %copy-start.7 = (bf16[1,16,16,256]{3,2,1,0:T(8,128)(2,1)S(1)}, bf16[1,16,16,256]{3,2,1,0:T(8,128)(2,1)}, u32[]{:S(2)}) copy-start(bf16[1,16,16,256]{3,2,1,0:T(8,128)(2,1)} %param.21) | copy-start | bytes 393220
  54.7 19.3 %collective-permute-start.1 = (bf16[1,16,256]{2,1,0:T(8,128)(2,1)}, bf16[1,16,256]{2,1,0:T(8,128)(2,1)}, u32[]{:S(2)}, u32[]{:S(2)}) collective-permute-start(bf16[1,16,256]{2,1,0:T(8,128)(2,1)} %get-tuple-element.93), channel_id=1, source_target_pairs={{2,0},{4,2},{6,4},{3,1},{5,3},{7,5},{10,8},{12,10},{14,12},{11,9},... | collective-permute-start | bytes 24584 | tf_op jit(solution)/shard_map/ppermute | solution.py:19
  56.0 18.0 %collective-permute-start = (bf16[1,16,256]{2,1,0:T(8,128)(2,1)}, bf16[1,16,256]{2,1,0:T(8,128)(2,1)}, u32[]{:S(2)}, u32[]{:S(2)}) collective-permute-start(bf16[1,16,256]{2,1,0:T(8,128)(2,1)} %get-tuple-element.92), channel_id=1, source_target_pairs={{0,2},{2,4},{4,6},{1,3},{3,5},{5,7},{8,10},{10,12},{12,14},{9,11},... | collective-permute-start | bytes 24584 | tf_op jit(solution)/shard_map/ppermute | solution.py:16
  61.7 17.3 %collective-permute-start.9 = (bf16[1,16,256]{2,1,0:T(8,128)(2,1)}, bf16[1,16,256]{2,1,0:T(8,128)(2,1)S(1)}, u32[]{:S(2)}, u32[]{:S(2)}) collective-permute-start(bf16[1,16,256]{2,1,0:T(8,128)(2,1)} %get-tuple-element.49), channel_id=1, source_target_pairs={{2,0},{4,2},{6,4},{3,1},{5,3},{7,5},{10,8},{12,10},{14,12},{11,9},... | collective-permute-start | bytes 24584 | tf_op jit(solution)/shard_map/ppermute | solution.py:19
  63.0 16.0 %collective-permute-start.8 = (bf16[1,16,256]{2,1,0:T(8,128)(2,1)}, bf16[1,16,256]{2,1,0:T(8,128)(2,1)S(1)}, u32[]{:S(2)}, u32[]{:S(2)}) collective-permute-start(bf16[1,16,256]{2,1,0:T(8,128)(2,1)} %get-tuple-element.48), channel_id=1, source_target_pairs={{0,2},{2,4},{4,6},{1,3},{3,5},{5,7},{8,10},{10,12},{12,14},{9,11},... | collective-permute-start | bytes 24584 | tf_op jit(solution)/shard_map/ppermute | solution.py:16
  67.8 2.3 %copy-start.4 = (bf16[2304,256]{1,0:T(8,128)(2,1)S(1)}, bf16[2304,256]{1,0:T(8,128)(2,1)}, u32[]{:S(2)}) copy-start(bf16[2304,256]{1,0:T(8,128)(2,1)} %param.20) | copy-start | bytes 3538948
  68.0 2.1 %copy-start.1 = (bf16[34,256,256]{2,1,0:T(8,128)(2,1)}, bf16[34,256,256]{2,1,0:T(8,128)(2,1)S(1)}, u32[]{:S(2)}) copy-start(bf16[34,256,256]{2,1,0:T(8,128)(2,1)S(1)} %constant_dynamic-update-slice_fusion) | copy-start | bytes 13369348
  74.7 7.8 %collective-permute-start.3 = (bf16[18,1,256]{2,1,0:T(2,128)(2,1)S(1)}, bf16[18,1,256]{2,1,0:T(2,128)(2,1)S(1)}, u32[]{:S(2)}, u32[]{:S(2)}) collective-permute-start(bf16[18,1,256]{2,1,0:T(2,128)(2,1)S(1)} %get-tuple-element.40), channel_id=1, source_target_pairs={{1,0},{3,2},{5,4},{7,6},{9,8},{11,10},{13,12},{15,14},{17,16},{19,... | collective-permute-start | bytes 27656 | tf_op jit(solution)/shard_map/ppermute | solution.py:19
  76.0 6.5 %collective-permute-start.2 = (bf16[18,1,256]{2,1,0:T(2,128)(2,1)S(1)}, bf16[18,1,256]{2,1,0:T(2,128)(2,1)S(1)}, u32[]{:S(2)}, u32[]{:S(2)}) collective-permute-start(bf16[18,1,256]{2,1,0:T(2,128)(2,1)S(1)} %get-tuple-element.41), channel_id=1, source_target_pairs={{0,1},{2,3},{4,5},{6,7},{8,9},{10,11},{12,13},{14,15},{16,17},{18,... | collective-permute-start | bytes 27656 | tf_op jit(solution)/shard_map/ppermute | solution.py:16
  79.1 17.6 %collective-permute-start.11 = (bf16[18,1,256]{2,1,0:T(2,128)(2,1)S(1)}, bf16[18,1,256]{2,1,0:T(2,128)(2,1)S(1)}, u32[]{:S(2)}, u32[]{:S(2)}) collective-permute-start(bf16[18,1,256]{2,1,0:T(2,128)(2,1)S(1)} %get-tuple-element.32), channel_id=1, source_target_pairs={{0,1},{2,3},{4,5},{6,7},{8,9},{10,11},{12,13},{14,15},{16,17},{18,... | collective-permute-start | bytes 27656 | tf_op jit(solution)/shard_map/ppermute | solution.py:16
  80.4 16.4 %collective-permute-start.10 = (bf16[18,1,256]{2,1,0:T(2,128)(2,1)S(1)}, bf16[18,1,256]{2,1,0:T(2,128)(2,1)S(1)}, u32[]{:S(2)}, u32[]{:S(2)}) collective-permute-start(bf16[18,1,256]{2,1,0:T(2,128)(2,1)S(1)} %get-tuple-element.33), channel_id=1, source_target_pairs={{1,0},{3,2},{5,4},{7,6},{9,8},{11,10},{13,12},{15,14},{17,16},{19,... | collective-permute-start | bytes 27656 | tf_op jit(solution)/shard_map/ppermute | solution.py:19
  83.4 2.7 %copy-start.9 = (bf16[256,256]{1,0:T(8,128)(2,1)S(1)}, bf16[256,256]{1,0:T(8,128)(2,1)}, u32[]{:S(2)}) copy-start(bf16[256,256]{1,0:T(8,128)(2,1)} %get-tuple-element.97) | copy-start | bytes 393220
  85.4 4.0 %copy-start.5 = (bf16[2304,256]{1,0:T(8,128)(2,1)S(1)}, bf16[2304,256]{1,0:T(8,128)(2,1)}, u32[]{:S(2)}) copy-start(bf16[2304,256]{1,0:T(8,128)(2,1)} %param.19) | copy-start | bytes 3538948
  90.0 15.8 %collective-permute-start.5 = (bf16[1,16,256]{2,1,0:T(8,128)(2,1)S(1)}, bf16[1,16,256]{2,1,0:T(8,128)(2,1)S(1)}, u32[]{:S(2)}, u32[]{:S(2)}) collective-permute-start(bf16[1,16,256]{2,1,0:T(8,128)(2,1)S(1)} %get-tuple-element.89), channel_id=1, source_target_pairs={{2,0},{4,2},{6,4},{3,1},{5,3},{7,5},{10,8},{12,10},{14,12},{11,9},... | collective-permute-start | bytes 24584 | tf_op jit(solution)/shard_map/ppermute | solution.py:19
  91.3 14.5 %collective-permute-start.4 = (bf16[1,16,256]{2,1,0:T(8,128)(2,1)S(1)}, bf16[1,16,256]{2,1,0:T(8,128)(2,1)S(1)}, u32[]{:S(2)}, u32[]{:S(2)}) collective-permute-start(bf16[1,16,256]{2,1,0:T(8,128)(2,1)S(1)} %get-tuple-element.88), channel_id=1, source_target_pairs={{0,2},{2,4},{4,6},{1,3},{3,5},{5,7},{8,10},{10,12},{12,14},{9,11},... | collective-permute-start | bytes 24584 | tf_op jit(solution)/shard_map/ppermute | solution.py:16
  96.9 1.3 copy-start.6
  98.2 14.9 %copy-start.2 = (bf16[34,256,256]{2,1,0:T(8,128)(2,1)S(1)}, bf16[34,256,256]{2,1,0:T(8,128)(2,1)}, u32[]{:S(2)}) copy-start(bf16[34,256,256]{2,1,0:T(8,128)(2,1)} %get-tuple-element.68) | copy-start | bytes 13369348
  98.7 11.4 %collective-permute-start.13 = (bf16[1,16,256]{2,1,0:T(8,128)(2,1)S(1)}, bf16[1,16,256]{2,1,0:T(8,128)(2,1)S(1)}, u32[]{:S(2)}, u32[]{:S(2)}) collective-permute-start(bf16[1,16,256]{2,1,0:T(8,128)(2,1)S(1)} %get-tuple-element.45), channel_id=1, source_target_pairs={{2,0},{4,2},{6,4},{3,1},{5,3},{7,5},{10,8},{12,10},{14,12},{11,9},... | collective-permute-start | bytes 24584 | tf_op jit(solution)/shard_map/ppermute | solution.py:19
  100.3 9.9 %collective-permute-start.12 = (bf16[1,16,256]{2,1,0:T(8,128)(2,1)S(1)}, bf16[1,16,256]{2,1,0:T(8,128)(2,1)S(1)}, u32[]{:S(2)}, u32[]{:S(2)}) collective-permute-start(bf16[1,16,256]{2,1,0:T(8,128)(2,1)S(1)} %get-tuple-element.44), channel_id=1, source_target_pairs={{0,2},{2,4},{4,6},{1,3},{3,5},{5,7},{8,10},{10,12},{12,14},{9,11},... | collective-permute-start | bytes 24584 | tf_op jit(solution)/shard_map/ppermute | solution.py:16
  105.8 7.1 %collective-permute-start.7 = (bf16[18,1,256]{2,1,0:T(2,128)(2,1)S(1)}, bf16[18,1,256]{2,1,0:T(2,128)(2,1)S(1)}, u32[]{:S(2)}, u32[]{:S(2)}) collective-permute-start(bf16[18,1,256]{2,1,0:T(2,128)(2,1)S(1)} %get-tuple-element.36), channel_id=1, source_target_pairs={{1,0},{3,2},{5,4},{7,6},{9,8},{11,10},{13,12},{15,14},{17,16},{19,... | collective-permute-start | bytes 27656 | tf_op jit(solution)/shard_map/ppermute | solution.py:19
  107.1 5.8 %collective-permute-start.6 = (bf16[18,1,256]{2,1,0:T(2,128)(2,1)S(1)}, bf16[18,1,256]{2,1,0:T(2,128)(2,1)S(1)}, u32[]{:S(2)}, u32[]{:S(2)}) collective-permute-start(bf16[18,1,256]{2,1,0:T(2,128)(2,1)S(1)} %get-tuple-element.37), channel_id=1, source_target_pairs={{0,1},{2,3},{4,5},{6,7},{8,9},{10,11},{12,13},{14,15},{16,17},{18,... | collective-permute-start | bytes 27656 | tf_op jit(solution)/shard_map/ppermute | solution.py:16
  110.2 4.3 %collective-permute-start.15 = (bf16[18,1,256]{2,1,0:T(2,128)(2,1)S(1)}, bf16[18,1,256]{2,1,0:T(2,128)(2,1)S(1)}, u32[]{:S(2)}, u32[]{:S(2)}) collective-permute-start(bf16[18,1,256]{2,1,0:T(2,128)(2,1)S(1)} %get-tuple-element.28), channel_id=1, source_target_pairs={{0,1},{2,3},{4,5},{6,7},{8,9},{10,11},{12,13},{14,15},{16,17},{18,... | collective-permute-start | bytes 27656 | tf_op jit(solution)/shard_map/ppermute | solution.py:16
  111.5 3.1 %collective-permute-start.14 = (bf16[18,1,256]{2,1,0:T(2,128)(2,1)S(1)}, bf16[18,1,256]{2,1,0:T(2,128)(2,1)S(1)}, u32[]{:S(2)}, u32[]{:S(2)}) collective-permute-start(bf16[18,1,256]{2,1,0:T(2,128)(2,1)S(1)} %get-tuple-element.29), channel_id=1, source_target_pairs={{1,0},{3,2},{5,4},{7,6},{9,8},{11,10},{13,12},{15,14},{17,16},{19,... | collective-permute-start | bytes 27656 | tf_op jit(solution)/shard_map/ppermute | solution.py:19
  114.8 1.3 copy-start.8

commit v4 on v3

--- a/solution.py
+++ b/solution.py
@@ -6,19 +6,6 @@
 from jax.sharding import PartitionSpec as P
 
 HIST = 15
-
-
-def extended(block, sides, width):
-    for axis, dim in sides:
-        count = lax.axis_size(axis)
-        forward = [(i, i + 1) for i in range(count - 1)]
-        backward = [(target, source) for source, target in forward]
-        low = lax.ppermute(
-            lax.slice_in_dim(block, block.shape[dim] - width, None, axis=dim), axis, forward
-        )
-        high = lax.ppermute(lax.slice_in_dim(block, 0, width, axis=dim), axis, backward)
-        block = jnp.concatenate([low, block, high], axis=dim)
-    return block
 
 
 def fetch_kernel(
@@ -216,29 +203,160 @@
     return out.reshape(HIST, height * width, channels)
 
 
-def tap_views(padded, height, width, mirror):
-    views = []
-    for row_tap in range(3):
-        for col_tap in range(3):
-            top = 2 - row_tap if mirror else row_tap
-            left = 2 - col_tap if mirror else col_tap
-            views.append(padded[top : top + height, left : left + width])
-    return jnp.stack(views).reshape(9, height * width, -1)
-
-
-def forward_patch(field):
-    padded = extended(field, (("row", 0), ("col", 1)), 1)
-    return tap_views(padded, field.shape[0], field.shape[1], False)
-
-
-def backward_patch(field):
-    padded = extended(field, (("row", 0), ("col", 1)), 1)
-    return tap_views(padded, field.shape[0], field.shape[1], True)
-
-
-def flipped(weight):
-    channels = weight.shape[1]
-    return weight.reshape(9, channels, channels).transpose(0, 2, 1)
+SIDES = [(down, right) for down in (-1, 0, 1) for right in (-1, 0, 1) if (down, right) != (0, 0)]
+
+
+def block_kernel(
+    joined, upstream, conv_one, conv_two, encoded, d_joined, act_views, hidden_views, d_conv1,
+    up_views, back_views, field, conv1, edge, sent, came, sems
+):
+    rows, cols = lax.axis_size("row"), lax.axis_size("col")
+    row, col = lax.axis_index("row"), lax.axis_index("col")
+    height, width = act_views.shape[1] - 2, act_views.shape[2]
+    cells, channels = joined.shape
+
+    def there(down, right):
+        first = jnp.logical_and(row + down >= 0, row + down < rows)
+        return jnp.logical_and(first, jnp.logical_and(col + right >= 0, col + right < cols))
+
+    peers = 0
+    for down, right in SIDES:
+        found = there(down, right)
+        peers = peers + found.astype(jnp.int32)
+
+        @pl.when(found)
+        def _(down=down, right=right):
+            pl.semaphore_signal(
+                pltpu.get_barrier_semaphore(),
+                inc=1,
+                device_id={"row": row + down, "col": col + right},
+                device_id_type=pl.DeviceIdType.MESH,
+            )
+
+    pl.semaphore_wait(pltpu.get_barrier_semaphore(), peers)
+    for index, (down, right) in enumerate(SIDES):
+
+        @pl.when(jnp.logical_not(there(-down, -right)))
+        def _(index=index):
+            for which in range(4):
+                came[which, index] = jnp.zeros_like(came[which, index])
+
+    def copies(which):
+        made = []
+        for index, (down, right) in enumerate(SIDES):
+            source = {-1: 0, 1: 1}.get(down, 2 if right < 0 else 3)
+            made.append(
+                pltpu.make_async_remote_copy(
+                    src_ref=sent.at[which, source],
+                    dst_ref=came.at[which, index],
+                    send_sem=sems.at[which, index, 0],
+                    recv_sem=sems.at[which, index, 1],
+                    device_id={"row": row + down, "col": col + right},
+                    device_id_type=pl.DeviceIdType.MESH,
+                )
+            )
+        return made
+
+    def line(which, place):
+        return field[which, place * width : (place + 1) * width, :]
+
+    def begin(which, value):
+        field[which] = value
+        sent[which, 0] = line(which, 0).astype(sent.dtype)
+        sent[which, 1] = line(which, height - 1).astype(sent.dtype)
+        for place in range(height):
+            here = line(which, place)
+            edge[0, place : place + 1, :] = here[0:1]
+            edge[1, place : place + 1, :] = here[width - 1 : width]
+        sent[which, 2] = edge[0].astype(sent.dtype)
+        sent[which, 3] = edge[1].astype(sent.dtype)
+        for copy, side in zip(copies(which), SIDES):
+            pl.when(there(*side))(copy.start)
+
+    def finish(which, views):
+        for copy, (down, right) in zip(copies(which), SIDES):
+            pl.when(there(-down, -right))(copy.wait_recv)
+
+        def got(down, right):
+            return came[which, SIDES.index((down, right))].astype(jnp.float32)
+
+        lefts, rights = got(0, 1), got(0, -1)
+        for place in range(height + 2):
+            if place == 0 or place == height + 1:
+                sign = 1 if place == 0 else -1
+                here = got(sign, 0)
+                before = got(sign, 1)[width - 1 : width]
+                after = got(sign, -1)[0:1]
+            else:
+                here = line(which, place - 1)
+                before = lefts[place - 1 : place]
+                after = rights[place - 1 : place]
+            views[0, place] = jnp.concatenate([before, here[: width - 1]], axis=0).astype(views.dtype)
+            views[1, place] = here.astype(views.dtype)
+            views[2, place] = jnp.concatenate([here[1:], after], axis=0).astype(views.dtype)
+
+    def convolve(views, weight, mirror):
+        total = None
+        for tap in range(9):
+            top, left = tap // 3, tap % 3
+            if mirror:
+                top, left = 2 - top, 2 - left
+            view = views[left, top : top + height].reshape(cells, channels)
+            block = weight[tap * channels : (tap + 1) * channels, :]
+            term = lax.dot_general(
+                view, block, (((1,), (1 if mirror else 0,)), ((), ())), preferred_element_type=jnp.float32
+            )
+            total = term if total is None else total + term
+        return total
+
+    begin(0, jnp.maximum(joined[...].astype(jnp.float32), 0.0))
+    begin(1, upstream[...].astype(jnp.float32))
+    finish(0, act_views)
+    conv1[...] = convolve(act_views, conv_one, False)
+    begin(2, jnp.maximum(conv1[...], 0.0).astype(jnp.bfloat16).astype(jnp.float32))
+    finish(1, up_views)
+    masked = jnp.where(conv1[...] > 0.0, convolve(up_views, conv_two, True), 0.0).astype(jnp.bfloat16)
+    d_conv1[...] = masked
+    begin(3, masked.astype(jnp.float32))
+    finish(2, hidden_views)
+    encoded[...] = (joined[...].astype(jnp.float32) + convolve(hidden_views, conv_two, False)).astype(
+        jnp.bfloat16
+    )
+    finish(3, back_views)
+    d_act = convolve(back_views, conv_one, True)
+    d_joined[...] = (
+        upstream[...].astype(jnp.float32) + jnp.where(joined[...].astype(jnp.float32) > 0.0, d_act, 0.0)
+    ).astype(jnp.bfloat16)
+    for which in range(4):
+        for copy, side in zip(copies(which), SIDES):
+            pl.when(there(*side))(copy.wait_send)
+
+
+def residual_block(joined, upstream, conv_one, conv_two, height, width):
+    cells, channels = joined.shape
+    flat = jax.ShapeDtypeStruct((cells, channels), jnp.bfloat16)
+    views = jax.ShapeDtypeStruct((3, height + 2, width, channels), jnp.bfloat16)
+    vmem = pl.BlockSpec(memory_space=pltpu.VMEM)
+    return pl.pallas_call(
+        block_kernel,
+        out_shape=(flat, flat, views, views, flat),
+        in_specs=[vmem] * 4,
+        out_specs=(vmem,) * 5,
+        scratch_shapes=[
+            pltpu.VMEM(views.shape, jnp.bfloat16),
+            pltpu.VMEM(views.shape, jnp.bfloat16),
+            pltpu.VMEM((4, cells, channels), jnp.float32),
+            pltpu.VMEM((cells, channels), jnp.float32),
+            pltpu.VMEM((2, height, channels), jnp.float32),
+            pltpu.VMEM((4, 4, width, channels), jnp.bfloat16),
+            pltpu.VMEM((4, 8, width, channels), jnp.bfloat16),
+            pltpu.SemaphoreType.DMA((4, 8, 2)),
+        ],
+        compiler_params=pltpu.CompilerParams(
+            collective_id=2, has_side_effects=True, vmem_limit_bytes=40 * 1024 * 1024
+        ),
+        name="block",
+    )(joined, upstream, conv_one, conv_two)
 
 
 def flip(index, bit):
@@ -246,7 +364,7 @@
 
 
 def gradient_kernel(
-    counts, lhs, rhs, out, term, near_out, near_in, far_out, far_in, last_out, last_in, clip_out, clip_in,
+    stacked, act_views, hidden_views, d_joined, d_conv1, upstream, out, term, near_out, near_in, far_out, far_in, last_out, last_in, clip_out, clip_in,
     near_sem, far_sem, last_sem, clip_sem
 ):
     clips = lax.axis_size("clip")
@@ -273,14 +391,20 @@
             device_id_type=pl.DeviceIdType.MESH,
         )
 
-    size = lhs.shape[2]
+    size = stacked.shape[2]
     lanes = term.shape[4]
     part_rows = term.shape[3]
+    height = act_views.shape[1] - 2
     index = 0
-    for group, count in enumerate(counts):
-        for _ in range(count):
+    for group, (count, right) in enumerate(((stacked.shape[0], d_joined), (9, d_conv1), (9, upstream))):
+        for spot in range(count):
+            if group == 0:
+                left = stacked[spot]
+            else:
+                views = act_views if group == 1 else hidden_views
+                left = views[spot % 3, spot // 3 : spot // 3 + height].reshape(right.shape)
             product = lax.dot_general(
-                lhs[index], rhs[group], (((0,), (0,)), ((), ())), preferred_element_type=jnp.float32
+                left, right[...], (((0,), (0,)), ((), ())), preferred_element_type=jnp.float32
             )
             start = index * size
             done = 0
@@ -373,22 +497,20 @@
         copy.wait_send()
 
 
-def gradients(groups):
-    lhs = jnp.concatenate([group[0] for group in groups], axis=0)
-    rhs = jnp.stack([group[1] for group in groups])
-    counts = tuple(group[0].shape[0] for group in groups)
+def gradients(*operands):
+    stacked = operands[0]
     clips = lax.axis_size("clip")
     rows = lax.axis_size("row")
-    total = lhs.shape[0] * lhs.shape[2]
+    total = (stacked.shape[0] + 18) * stacked.shape[2]
     part_rows = total // (2 * clips * rows)
-    lanes = rhs.shape[2] // lax.axis_size("col")
+    lanes = stacked.shape[2] // lax.axis_size("col")
     piece = (part_rows, lanes)
     vmem = pl.BlockSpec(memory_space=pltpu.VMEM)
     dma = pltpu.SemaphoreType.DMA
     out = pl.pallas_call(
-        lambda *refs: gradient_kernel(counts, *refs),
+        gradient_kernel,
         out_shape=jax.ShapeDtypeStruct((2,) + piece, jnp.float32),
-        in_specs=[vmem, vmem],
+        in_specs=[vmem] * 6,
         out_specs=vmem,
         scratch_shapes=[
             pltpu.VMEM((2, clips * rows, 2) + piece, jnp.float32),
@@ -409,7 +531,7 @@
             collective_id=1, has_side_effects=True, vmem_limit_bytes=48 * 1024 * 1024
         ),
         name="gradients",
-    )(lhs, rhs)
+    )(*operands)
     return out.reshape(2 * part_rows, lanes)
 
 
@@ -434,35 +556,12 @@
     joined = jnp.einsum(
         "kpc,kcd->pd", stacked, join_blocks, preferred_element_type=jnp.float32
     ).astype(jnp.bfloat16)
-    act = jnp.maximum(joined, 0)
-    act_patch = forward_patch(act.reshape(height, width, channels))
-    conv1 = jnp.einsum("tpc,tcd->pd", act_patch, conv_one.reshape(9, channels, channels), preferred_element_type=jnp.float32)
-    hidden = jnp.maximum(conv1, 0.0).astype(jnp.bfloat16)
-    hidden_patch = forward_patch(hidden.reshape(height, width, channels))
-    conv2 = jnp.einsum("tpc,tcd->pd", hidden_patch, conv_two.reshape(9, channels, channels), preferred_element_type=jnp.float32)
-    encoded = (
-        (joined.astype(jnp.float32) + conv2)
-        .astype(jnp.bfloat16)
-        .reshape(1, height, width, channels)
+    upstream = grad_out.reshape(cells, channels)
+    encoded, d_joined, act_views, hidden_views, d_conv1 = residual_block(
+        joined, upstream, conv_one, conv_two, height, width
     )
-    upstream = grad_out[0]
-    flat_up = upstream.reshape(cells, channels)
-    d_hidden = jnp.einsum(
-        "tpc,tcd->pd", backward_patch(upstream), flipped(conv_two), preferred_element_type=jnp.float32
-    )
-    d_conv1 = jnp.where(conv1 > 0, d_hidden, 0.0).astype(jnp.bfloat16)
-    d_act = jnp.einsum(
-        "tpc,tcd->pd",
-        backward_patch(d_conv1.reshape(height, width, channels)),
-        flipped(conv_one),
-        preferred_element_type=jnp.float32,
-    )
-    d_joined = (flat_up.astype(jnp.float32) + jnp.where(joined > 0, d_act, 0.0)).astype(
-        jnp.bfloat16
-    )
-    weight_grads = gradients(
-        ((stacked, d_joined), (act_patch, d_conv1), (hidden_patch, flat_up))
-    )
+    encoded = encoded.reshape(1, height, width, channels)
+    weight_grads = gradients(stacked, act_views, hidden_views, d_joined, d_conv1, upstream)
     return (encoded, weight_grads)
 
 

time: 155 us -> 106 us (0.68)
  starting transfers between devices: 40 us -> 0 us
  local copies, waits for them, and re-layouts: 17.7 us -> 5.69 us
  Pallas kernels: 85.9 us -> 97.1 us
  other arithmetic: 5.43 us -> 1.89 us
  matrix products: 3.94 us -> 0.72 us
    ppermute x16 -> x0, starting transfers between devices: 40 us -> none  [the longest x8 29.4 us: extended(): lax.ppermute(lax.slice_in_dim(block, block.shape[dim] - width, None, axis...]
    pallas_call x1 -> x2, Pallas kernels: 37.1 us -> 48.3 us  [the longest x1 36 us: gradients(): pl.pallas_call(gradient_kernel, out_shape=jax.ShapeDtypeStruct((2,) + pie...]
    unnamed x57 -> x14, local copies, waits for them, and re-layouts: 12.1 us -> 5.6 us
    reshape x2 -> x0, local copies, waits for them, and re-layouts: 3.9 us -> none  [the longest x1 2.37 us: local(): conv_one.reshape(9, channels, channels)]
    concatenate x12 -> x1, other arithmetic: 2.85 us -> 0.18 us  [local(): jnp.concatenate([current.reshape(1, cells, channels), warped], axis=0)]
    dot_general x4 -> x0, matrix products: 2.57 us -> none  [the longest x1 1.14 us: local(): jnp.einsum('tpc,tcd->pd', hidden_patch, conv_two.reshape(9, channels, cha...]
  transfers between devices with their start and end apart: 16 -> 0, of which waited for: 1 -> 0; matrix products, arithmetic and copies ran while one was open for 10% -> 0% of each run, Pallas kernels for 0% -> 0%
where the time goes in v4:
time: 106 us
  Pallas kernels  97.1 us (92%)
  local copies, waits for them, and re-layouts  5.69 us (5%)
  other arithmetic  1.89 us (2%)
    pallas_call x1, Pallas kernels, fetch(): pl.pallas_call(fetch_kernel, out_shape=jax.ShapeDtypeStruct((HIST, 2) + h...  48.8 us
    pallas_call x1, Pallas kernels, gradients(): pl.pallas_call(gradient_kernel, out_shape=jax.ShapeDtypeStruct((2,) + pie...  36 us
    pallas_call x1, Pallas kernels, residual_block(): pl.pallas_call(block_kernel, out_shape=(flat, flat, views, views, flat),...  12.3 us
    unnamed x14, local copies, waits for them, and re-layouts  5.6 us

profile of v4, /device:TPU:0, one launch (start us, length us, event | category | flops | bytes accessed | tf_op | source)
XLA Modules:
  0.0 106.1 jit_solution(14097815921629842844)
XLA Ops:
  0.6 0.0 copy-start
  0.7 1.6 %copy-done = bf16[4096,256]{1,0:T(8,128)(2,1)S(1)} copy-done((bf16[4096,256]{1,0:T(8,128)(2,1)S(1)}, bf16[4096,256]{1,0:T(8,128)(2,1)}, u32[]{:S(2)}) %copy-start) | copy-done | bytes 2097176
  2.2 0.8 convert_add_fusion
  3.0 0.9 select_reduce_fusion
  3.9 0.1 reshape.33.served
  4.0 0.0 copy-start.3
  4.0 1.2 %copy-done.3 = bf16[1,8,16,16,256]{4,3,2,1,0:T(8,128)(2,1)S(1)} copy-done((bf16[1,8,16,16,256]{4,3,2,1,0:T(8,128)(2,1)S(1)}, bf16[1,8,16,16,256]{4,3,2,1,0:T(8,128)(2,1)}, u32[]{:S(2)}) %copy-start.3) | copy-done | bytes 1048600
  5.3 0.0 copy-start.5
  5.3 48.8 %fetch.1 = bf16[15,2,8,2,8,256]{5,4,3,2,1,0:T(8,128)(2,1)S(1)} custom-call(s32[16]{0:T(128)S(1)} %reshape.33.served, s32[15]{0:T(128)S(1)} %dynamic-slice_bitcast_fusion.wanted, bf16[8,2,8,2,8,256]{5,4,3,2,1,0:T(8,128)(2,1)S(1)} %bitcast.18), custom_call_target="tpu_custom_call" | custom-call | tf_op jit(solution)/shard_map/fetch/pallas_call | solution.py:182
  54.1 0.0 copy-done.5
  54.1 0.7 fusion.joined
  54.8 0.0 copy-start.1
  54.8 0.0 copy-start.2
  54.8 0.0 copy-start.4
  54.8 0.2 pad_maximum_fusion.stacked
  55.0 1.0 copy-done.1
  56.1 0.4 copy-done.2
  56.4 0.0 copy-done.4
  56.4 12.3 %block.1 = (bf16[256,256]{1,0:T(8,128)(2,1)S(1)}, bf16[256,256]{1,0:T(8,128)(2,1)S(1)}, bf16[3,18,16,256]{3,2,1,0:T(8,128)(2,1)S(1)}, bf16[3,18,16,256]{3,2,1,0:T(8,128)(2,1)S(1)}, bf16[256,256]{1,0:T(8,128)(2,1)S(1)}) custom-call(bf16[256,256]{1,0:T(8,128)(2,1)S(1)} %fusion.joined, bf16[256,256]{1,0:T(8,128)(2,1)S(1)} %bitcast.19, ...), custom_call_target="tpu_custom_call" | custom-call | tf_op jit(solution)/shard_map/block/pallas_call | solution.py:340
  68.7 36.0 %gradients.1 = f32[2,272,128]{2,1,0:T(8,128)S(1)} custom-call(bf16[16,256,256]{2,1,0:T(8,128)(2,1)S(1)} %pad_maximum_fusion.stacked, bf16[3,18,16,256]{3,2,1,0:T(8,128)(2,1)S(1)} %get-tuple-element.8.act_views, bf16[3,18,16,256]{3,2,1,0:T(8,128)(2,1)S(1)} %get-tuple-element.9.hidden_views, bf16[256,256]{1,0:T(8,128)(2,1)S(1)} %get-tuple-element.10.d_joined, ...), custom_call_target="tpu_custom_call" | custom-call | tf_op jit(solution)/shard_map/gradients/pallas_call | solution.py:510
  104.7 0.7 copy.15
  105.4 0.7 copy.16
  (2 shorter events, 0.0 us)
Async XLA Ops:
  0.6 1.6 %copy-start = (bf16[4096,256]{1,0:T(8,128)(2,1)S(1)}, bf16[4096,256]{1,0:T(8,128)(2,1)}, u32[]{:S(2)}) copy-start(bf16[4096,256]{1,0:T(8,128)(2,1)} %param.18) | copy-start | bytes 6291460
  4.0 1.2 %copy-start.3 = (bf16[1,8,16,16,256]{4,3,2,1,0:T(8,128)(2,1)S(1)}, bf16[1,8,16,16,256]{4,3,2,1,0:T(8,128)(2,1)}, u32[]{:S(2)}) copy-start(bf16[1,8,16,16,256]{4,3,2,1,0:T(8,128)(2,1)} %param.12) | copy-start | bytes 3145732
  5.3 48.8 %copy-start.5 = (bf16[1,16,16,256]{3,2,1,0:T(8,128)(2,1)S(1)}, bf16[1,16,16,256]{3,2,1,0:T(8,128)(2,1)}, u32[]{:S(2)}) copy-start(bf16[1,16,16,256]{3,2,1,0:T(8,128)(2,1)} %param.11) | copy-start | bytes 393220
  54.8 1.3 %copy-start.1 = (bf16[2304,256]{1,0:T(8,128)(2,1)S(1)}, bf16[2304,256]{1,0:T(8,128)(2,1)}, u32[]{:S(2)}) copy-start(bf16[2304,256]{1,0:T(8,128)(2,1)} %conv_one.1) | copy-start | bytes 3538948
  54.8 1.6 %copy-start.2 = (bf16[2304,256]{1,0:T(8,128)(2,1)S(1)}, bf16[2304,256]{1,0:T(8,128)(2,1)}, u32[]{:S(2)}) copy-start(bf16[2304,256]{1,0:T(8,128)(2,1)} %conv_two.1) | copy-start | bytes 3538948
  54.8 1.6 %copy-start.4 = (bf16[1,16,16,256]{3,2,1,0:T(8,128)(2,1)S(1)}, bf16[1,16,16,256]{3,2,1,0:T(8,128)(2,1)}, u32[]{:S(2)}) copy-start(bf16[1,16,16,256]{3,2,1,0:T(8,128)(2,1)} %param.21) | copy-start | bytes 393220

commit v5 on v4

--- a/solution.py
+++ b/solution.py
@@ -9,7 +9,8 @@
 
 
 def fetch_kernel(
-    served, wanted, bank, out, own, rim, chosen, got, near_sem, row_sem, col_sem, clip_sem, local_sem
+    request, picks, shift_rows, shift_cols, counts, bank, out, table, core, own, rim, chosen, got,
+    near_sem, row_sem, col_sem, clip_sem, local_sem
 ):
     frames = bank.shape[0]
     clips = lax.axis_size("clip")
@@ -36,7 +37,9 @@
             device_id_type=pl.DeviceIdType.MESH,
         )
 
-    centre = pltpu.make_async_copy(bank, own.at[0:frames, :, :, 1:3], local_sem)
+    inner = pltpu.make_async_copy(bank, core.at[0:frames], local_sem.at[0])
+    inner.start()
+    centre = pltpu.make_async_copy(bank, own.at[0:frames, :, :, 1:3], local_sem.at[1])
     centre.start()
     partners = [lax.rem(clip + step, clips) for step in range(1, clips)]
     for partner in partners:
@@ -62,35 +65,23 @@
     pl.when(down)(to_down.start)
     pl.when(up)(to_up.start)
 
-    own[frames] = jnp.zeros_like(own[frames])
-    rim[frames] = jnp.zeros_like(rim[frames])
-
-    def clear(view, place):
-        for frame in range(frames):
-            view[(frame,) + place] = jnp.zeros_like(view[(frame,) + place])
-
-    every = slice(None)
-    pl.when(jnp.logical_not(up))(lambda: clear(rim, (0,)))
-    pl.when(jnp.logical_not(down))(lambda: clear(rim, (2,)))
-
-    @pl.when(jnp.logical_not(left))
-    def _():
-        clear(own, (every, every, 0))
-        clear(rim, (0, every, 0))
-        clear(rim, (2, every, 0))
-
-    @pl.when(jnp.logical_not(right))
-    def _():
-        clear(own, (every, every, 3))
-        clear(rim, (0, every, 3))
-        clear(rim, (2, every, 3))
-
-    centre.wait()
-    pl.when(left)(to_right.wait_recv)
-    pl.when(right)(to_left.wait_recv)
+    core[frames] = jnp.zeros_like(core[frames])
+
+    def match(slot, carry):
+        partner = lax.div(slot, capacity)
+        target = clip * capacity + lax.rem(slot, capacity)
+        found = jnp.int32(0)
+        for spot in range(out.shape[0]):
+            frame = jnp.where(spot < counts[partner], picks[partner, spot], frames)
+            packed = (frame * 3 + shift_rows[partner, spot] + 1) * 3 + shift_cols[partner, spot] + 1
+            found = jnp.where(request[partner, spot] == target, packed, found)
+        table[slot] = found
+        return carry
+
+    lax.fori_loop(0, clips * capacity, match, 0)
 
     def decode(slot):
-        packed = served[slot]
+        packed = table[slot]
         shift_col = lax.rem(packed, 3) - 1
         rest = lax.div(packed, 3)
         return lax.div(rest, 3), lax.rem(rest, 3) - 1, shift_col
@@ -99,11 +90,15 @@
         for spot in range(capacity):
             slot = partner * capacity + spot
             frame, shift_row, shift_col = decode(slot)
+            line = jnp.where(shift_row < 0, 1, 0)
+            near = jnp.where(shift_col < 0, 1, 0)
+            away = jnp.where(shift_col == 0, 2, jnp.where(shift_col > 0, 0, 3))
             if part == 0:
-                line = jnp.where(shift_row < 0, 1, 0)
-                target[0, slot] = own[frame, line, :, pl.ds(1 - shift_col, 2)]
+                target[0, slot] = core[frame, line, :, near]
+            elif part == 1:
+                target[1, slot] = own[frame, line, :, away]
             else:
-                target[1, slot] = rim[frame, 1 - shift_row, :, pl.ds(1 - shift_col, 2)]
+                target[part, slot] = rim[frame, 1 - shift_row, :, near + 1 if part == 2 else away]
 
     sends = []
 
@@ -117,8 +112,45 @@
         copy.start()
         sends.append(copy)
 
-    for part in range(2):
-        if part == 1:
+    def serve(part):
+        for step in range(1, clips):
+            pick(part, chosen, partners[step - 1])
+            if step > 1:
+                send(part, step - 1)
+        pick(part, got, clip)
+        send(part, clips - 1)
+
+    inner.wait()
+    serve(0)
+    own[frames] = jnp.zeros_like(own[frames])
+    rim[frames] = jnp.zeros_like(rim[frames])
+
+    def clear(view, place):
+        for frame in range(frames):
+            view[(frame,) + place] = jnp.zeros_like(view[(frame,) + place])
+
+    every = slice(None)
+    pl.when(jnp.logical_not(up))(lambda: clear(rim, (0,)))
+    pl.when(jnp.logical_not(down))(lambda: clear(rim, (2,)))
+
+    @pl.when(jnp.logical_not(left))
+    def _():
+        clear(own, (every, every, 0))
+        clear(rim, (0, every, 0))
+        clear(rim, (2, every, 0))
+
+    @pl.when(jnp.logical_not(right))
+    def _():
+        clear(own, (every, every, 3))
+        clear(rim, (0, every, 3))
+        clear(rim, (2, every, 3))
+
+    centre.wait()
+    pl.when(left)(to_right.wait_recv)
+    pl.when(right)(to_left.wait_recv)
+
+    for part in range(1, 4):
+        if part == 2:
             def keep(frame, carry):
                 rim[frame, 1] = own[frame, 1]
                 return carry
@@ -136,21 +168,19 @@
                 pl.when(jnp.logical_and(vertical, side))(copy.start)
             for (vertical, _, copy), other in zip(corners, (left, left, right, right)):
                 pl.when(jnp.logical_and(vertical, other))(copy.wait_recv)
-        for step in range(1, clips):
-            pick(part, chosen, partners[step - 1])
-            if step > 1:
-                send(part, step - 1)
-        pick(part, got, clip)
-        send(part, clips - 1)
+        serve(part)
     for copy in sends:
         copy.wait_recv()
     slots = out.shape[0]
     for slot in range(slots):
-        packed = wanted[slot]
-        place = lax.div(packed, 2)
-        flag = lax.rem(packed, 2)
-        out[slot, 0] = got[flag, place]
-        out[slot, 1] = got[1 - flag, place]
+        place = request[clip, slot]
+        below = jnp.where(shift_rows[clip, slot] > 0, 1, 0)
+        beside = jnp.where(shift_cols[clip, slot] > 0, 1, 0)
+        for line in range(2):
+            for lane in range(2):
+                first = 1 - below if line else below
+                second = 1 - beside if lane else beside
+                out[slot, line, :, lane] = got[2 * first + second, place]
     for copy in sends:
         copy.wait_send()
     pl.when(right)(to_right.wait_send)
@@ -165,15 +195,6 @@
     frames, height, width, channels = bank.shape
     clips = lax.axis_size("clip")
     capacity = (HIST + clips - 1) // clips
-    own_clip = lax.axis_index("clip")
-    slot_ids = own_clip * capacity + jnp.arange(capacity, dtype=jnp.int32)
-    matches = (request[:, None, :] == slot_ids[None, :, None]).astype(jnp.int32)
-    valid = jnp.arange(HIST)[None, :] < hist_count[:, None]
-    frame = jnp.where(valid, frame_pick, frames)
-    packed = (frame * 3 + shift_rows + 1) * 3 + shift_cols + 1
-    served = jnp.sum(matches * packed[:, None, :], axis=-1).reshape(-1)
-    pair = request * 2 + (shift_rows == 1).astype(jnp.int32)
-    wanted = lax.dynamic_index_in_dim(pair, own_clip, 0, False)
     half = (height // 2, 2, width // 2, channels)
     blocks = bank.reshape((frames, 2) + half)
     wide = (height // 2, 4, width // 2, channels)
@@ -182,24 +203,26 @@
     out = pl.pallas_call(
         fetch_kernel,
         out_shape=jax.ShapeDtypeStruct((HIST, 2) + half, bank.dtype),
-        in_specs=[smem, smem, pl.BlockSpec(memory_space=pl.ANY)],
+        in_specs=[smem] * 5 + [pl.BlockSpec(memory_space=pl.ANY)],
         out_specs=pl.BlockSpec(memory_space=pltpu.VMEM),
         scratch_shapes=[
+            pltpu.SMEM((clips * capacity,), jnp.int32),
+            pltpu.VMEM((frames + 1, 2) + half, bank.dtype),
             pltpu.VMEM((frames + 1, 2) + wide, bank.dtype),
             pltpu.VMEM((frames + 1, 3) + wide, bank.dtype),
-            pltpu.VMEM((2, clips * capacity) + half, bank.dtype),
-            pltpu.VMEM((2, clips * capacity) + half, bank.dtype),
+            pltpu.VMEM((4, clips * capacity, height // 2, width // 2, channels), bank.dtype),
+            pltpu.VMEM((4, clips * capacity, height // 2, width // 2, channels), bank.dtype),
             dma((2, 2)),
             dma((2, 2)),
             dma((4, 2)),
-            dma((2, clips - 1, 2)),
-            dma,
+            dma((4, clips - 1, 2)),
+            dma((2,)),
         ],
         compiler_params=pltpu.CompilerParams(
             collective_id=0, has_side_effects=True, vmem_limit_bytes=40 * 1024 * 1024
         ),
         name="fetch",
-    )(served, wanted, blocks)
+    )(request, frame_pick, shift_rows, shift_cols, hist_count, blocks)
     return out.reshape(HIST, height * width, channels)
 
 

time: 106 us -> 108 us (1.019)
  local copies, waits for them, and re-layouts: 5.69 us -> 8.98 us
  other arithmetic: 1.89 us -> 0.18 us
    unnamed x14 -> x24, local copies, waits for them, and re-layouts: 5.6 us -> 8.98 us
    pallas_call x1, Pallas kernels: 48.8 us -> 52 us  [fetch(): pl.pallas_call(fetch_kernel, out_shape=jax.ShapeDtypeStruct((HIST, 2) + h...]
    pallas_call x1, Pallas kernels: 36 us -> 33.2 us  [gradients(): pl.pallas_call(gradient_kernel, out_shape=jax.ShapeDtypeStruct((2,) + pie...]
where the time goes in v5:
time: 108 us
  Pallas kernels  97.4 us (90%)
  local copies, waits for them, and re-layouts  8.98 us (8%)
    pallas_call x1, Pallas kernels, fetch(): pl.pallas_call(fetch_kernel, out_shape=jax.ShapeDtypeStruct((HIST, 2) + h...  52 us
    pallas_call x1, Pallas kernels, gradients(): pl.pallas_call(gradient_kernel, out_shape=jax.ShapeDtypeStruct((2,) + pie...  33.2 us
    pallas_call x1, Pallas kernels, residual_block(): pl.pallas_call(block_kernel, out_shape=(flat, flat, views, views, flat),...  12.3 us
    unnamed x24, local copies, waits for them, and re-layouts  8.98 us

profile of v5, /device:TPU:0, one launch (start us, length us, event | category | flops | bytes accessed | tf_op | source)
XLA Modules:
  0.0 108.0 jit_solution(8268551528403981846)
XLA Ops:
  0.6 0.0 copy-start
  0.6 1.6 %copy-done = bf16[4096,256]{1,0:T(8,128)(2,1)S(1)} copy-done((bf16[4096,256]{1,0:T(8,128)(2,1)S(1)}, bf16[4096,256]{1,0:T(8,128)(2,1)}, u32[]{:S(2)}) %copy-start) | copy-done | bytes 2097176
  2.2 0.0 copy-start.3
  2.2 1.2 %copy-done.3 = bf16[1,8,16,16,256]{4,3,2,1,0:T(8,128)(2,1)S(1)} copy-done((bf16[1,8,16,16,256]{4,3,2,1,0:T(8,128)(2,1)S(1)}, bf16[1,8,16,16,256]{4,3,2,1,0:T(8,128)(2,1)}, u32[]{:S(2)}) %copy-start.3) | copy-done | bytes 1048600
  3.5 0.0 copy-start.5
  3.5 0.7 copy-done.5
  4.1 0.0 copy-start.6
  4.1 0.7 copy-done.6
  4.8 0.0 copy-start.7
  4.8 0.7 copy-done.7
  5.5 0.0 copy-start.8
  5.5 0.7 copy-done.8
  6.2 0.0 copy-start.9
  6.2 0.7 copy-done.9
  6.8 0.0 copy-start.10
  6.8 52.0 %fetch.1 = bf16[15,2,8,2,8,256]{5,4,3,2,1,0:T(8,128)(2,1)S(1)} custom-call(s32[4,15]{1,0:T(4,128)S(1)} %copy-done.5, s32[4,15]{1,0:T(4,128)S(1)} %copy-done.6, s32[4,15]{1,0:T(4,128)S(1)} %copy-done.7, s32[4,15]{1,0:T(4,128)S(1)} %copy-done.8, s32[4]{0:T(128)S(1)} %copy-done.9, bf16[8,2,8,2,8,256]{5,4,3,2,1,0:T(8,128)(2,1)S(1)} %bitcast.16), custom_call_target="tpu_custom_call" | custom-call | tf_op jit(solution)/shard_map/fetch/pallas_call | solution.py:203
  58.8 0.0 copy-done.10
  58.8 0.7 fusion.joined
  59.6 0.0 copy-start.1
  59.6 0.0 copy-start.2
  59.6 0.0 copy-start.4
  59.6 0.2 pad_maximum_fusion.stacked
  59.8 1.0 copy-done.1
  60.8 0.4 copy-done.2
  61.2 0.0 copy-done.4
  61.2 12.3 %block.1 = (bf16[256,256]{1,0:T(8,128)(2,1)S(1)}, bf16[256,256]{1,0:T(8,128)(2,1)S(1)}, bf16[3,18,16,256]{3,2,1,0:T(8,128)(2,1)S(1)}, bf16[3,18,16,256]{3,2,1,0:T(8,128)(2,1)S(1)}, bf16[256,256]{1,0:T(8,128)(2,1)S(1)}) custom-call(bf16[256,256]{1,0:T(8,128)(2,1)S(1)} %fusion.joined, bf16[256,256]{1,0:T(8,128)(2,1)S(1)} %bitcast.17, ...), custom_call_target="tpu_custom_call" | custom-call | tf_op jit(solution)/shard_map/block/pallas_call | solution.py:363
  73.5 33.2 %gradients.1 = f32[2,272,128]{2,1,0:T(8,128)S(1)} custom-call(bf16[16,256,256]{2,1,0:T(8,128)(2,1)S(1)} %pad_maximum_fusion.stacked, bf16[3,18,16,256]{3,2,1,0:T(8,128)(2,1)S(1)} %get-tuple-element.8.act_views, bf16[3,18,16,256]{3,2,1,0:T(8,128)(2,1)S(1)} %get-tuple-element.9.hidden_views, bf16[256,256]{1,0:T(8,128)(2,1)S(1)} %get-tuple-element.10.d_joined, ...), custom_call_target="tpu_custom_call" | custom-call | tf_op jit(solution)/shard_map/gradients/pallas_call | solution.py:533
  106.6 0.7 copy.15
  107.3 0.7 copy.16
Async XLA Ops:
  0.6 1.6 %copy-start = (bf16[4096,256]{1,0:T(8,128)(2,1)S(1)}, bf16[4096,256]{1,0:T(8,128)(2,1)}, u32[]{:S(2)}) copy-start(bf16[4096,256]{1,0:T(8,128)(2,1)} %param.18) | copy-start | bytes 6291460
  2.2 1.2 %copy-start.3 = (bf16[1,8,16,16,256]{4,3,2,1,0:T(8,128)(2,1)S(1)}, bf16[1,8,16,16,256]{4,3,2,1,0:T(8,128)(2,1)}, u32[]{:S(2)}) copy-start(bf16[1,8,16,16,256]{4,3,2,1,0:T(8,128)(2,1)} %param.12) | copy-start | bytes 3145732
  3.5 0.7 copy-start.5
  4.1 0.7 copy-start.6
  4.8 0.7 copy-start.7
  5.5 0.7 copy-start.8
  6.2 0.7 copy-start.9
  6.8 52.0 %copy-start.10 = (bf16[1,16,16,256]{3,2,1,0:T(8,128)(2,1)S(1)}, bf16[1,16,16,256]{3,2,1,0:T(8,128)(2,1)}, u32[]{:S(2)}) copy-start(bf16[1,16,16,256]{3,2,1,0:T(8,128)(2,1)} %param.11) | copy-start | bytes 393220
  59.6 1.3 %copy-start.1 = (bf16[2304,256]{1,0:T(8,128)(2,1)S(1)}, bf16[2304,256]{1,0:T(8,128)(2,1)}, u32[]{:S(2)}) copy-start(bf16[2304,256]{1,0:T(8,128)(2,1)} %conv_one.1) | copy-start | bytes 3538948
  59.6 1.6 %copy-start.2 = (bf16[2304,256]{1,0:T(8,128)(2,1)S(1)}, bf16[2304,256]{1,0:T(8,128)(2,1)}, u32[]{:S(2)}) copy-start(bf16[2304,256]{1,0:T(8,128)(2,1)} %conv_two.1) | copy-start | bytes 3538948
  59.6 1.6 %copy-start.4 = (bf16[1,16,16,256]{3,2,1,0:T(8,128)(2,1)S(1)}, bf16[1,16,16,256]{3,2,1,0:T(8,128)(2,1)}, u32[]{:S(2)}) copy-start(bf16[1,16,16,256]{3,2,1,0:T(8,128)(2,1)} %param.21) | copy-start | bytes 393220
